TPU v7x, 256 devices: a whole 4x4x8 slice. The times are simulated.
256 devices in a mesh: rows: 16 (over z_lo, y, core), cols: 16 (over x, z_hi).
Axes of the slice: x: 4, y: 4, z: 8 (z_hi: 4, z_lo: 2; z = z_hi * 2 + z_lo), core: 2. Of those that a mesh axis runs over, the one named last changes fastest.
Arguments:
- displacement: float32 [16384, 288], P(('rows', 'cols')), may hold values from -6 to 6
- positions: float32 [16384, 288], P(('rows', 'cols')), as said below
- cluster_basis: bfloat16 [16384, 288, 64], P(('rows', 'cols')), may hold values from -0.375 to 0.375
- near_pairs: int32 [65536, 2], P(('rows', 'cols')), may hold values from 0 to 67, as said below
- near_count: int32 [256], P(('rows', 'cols')), may hold values from 64 to 256, as said below
- far_pairs: int32 [262144, 2], P(('rows', 'cols')), may hold values from 0 to 1023, as said below
- far_count: int32 [256], P(('rows', 'cols')), may hold values from 256 to 1024, as said below
- far_blocks: bfloat16 [262144, 64, 64], P(('rows', 'cols')), may hold values from -0.75 to 0.75
- intact: int32 [16384, 96], P(('rows', 'cols')), may hold values 0 or 1
- stiffness: float32 [16384, 96], P(('rows', 'cols')), may hold values from 0.5 to 2
Outputs:
- net_traction: float32 [16384, 288], P(('rows', 'cols'))
- damage: float32 [16384, 96], P(('rows', 'cols'))
Inputs may be any that keep to these rules, and one draw needn't show every extreme that they name: `positions`: centroids of the elements of each cluster. `near_pairs`: column 0 is a cluster of the device's own 64; column 1 counts from 2 clusters before the device's first cluster and names a cluster at most 2 away from the target in the cluster order. Dead slots hold valid entries too. `near_count`: loads differ from device to device. `far_pairs`: column 0 is a target cluster of the device's index along rows (0 to 1023); column 1 a source cluster of its index along cols (0 to 1023), numbered through the devices of that column in the order of rows. Dead slots hold valid entries too. `far_count`: loads differ from device to device.
All inputs are finite; a program needn't handle non-finite values. No bound on the sum of `intact` on one device may be relied on, other than what follows from the above.
Results may differ from a plain program's by a relative error of at most 0.0014.
Values may be sent and summed in bfloat16 or wider, within the bound.
A program may use at most 128 MiB of HBM per device.

v0:
```python
import jax
import jax.numpy as jnp
from jax import lax
from jax.sharding import PartitionSpec as P

HALO = 2


core_square = 0.25
softening = 1.5
pair_group = 32


def with_halo(array, sides, width):
    for axis, dim in sides:
        devices, length = (lax.axis_size(axis), array.shape[dim])
        up = [(i, (i + 1) % devices) for i in range(devices - 1)]
        down = [(j, i) for i, j in up]
        last = lax.slice_in_dim(array, length - width, length, axis=dim)
        leading = lax.slice_in_dim(array, 0, width, axis=dim)
        before = lax.ppermute(last, axis, up)
        after = lax.ppermute(leading, axis, down)
        array = jnp.concatenate([before, array, after], axis=dim)
    return array


def kernel_block(target_pos, source_pos, source_disp):
    offsets = target_pos[:, :, :, None] - source_pos[:, :, None, :]
    distance = jnp.sum(offsets * offsets, axis=1) + core_square
    inverse = lax.rsqrt(distance)
    inverse = inverse * inverse * inverse
    along = jnp.sum(offsets * source_disp[:, :, None, :], axis=1)
    direct = jnp.sum(inverse[:, None, :, :] * source_disp[:, :, None, :], axis=3)
    second = jnp.sum(offsets * (along * inverse / distance)[:, None, :, :], axis=3)
    return direct - 3.0 * second


def local(
    displacement,
    positions,
    cluster_basis,
    near_pairs,
    near_count,
    far_pairs,
    far_count,
    far_blocks,
    intact,
    stiffness,
):
    clusters = displacement.shape[0]
    row_width = displacement.shape[1]
    elems = row_width // 3
    stacked = jnp.stack([displacement, positions])
    extended = with_halo(stacked, ((("rows", "cols"), 1),), HALO)
    ext_disp = extended[0]
    ext_pos = extended[1]
    near_slots = near_pairs.shape[0]
    group_size = min(pair_group, near_slots)

    def near_step(group_index, summed):
        first_slot = group_index * group_size
        chosen = lax.dynamic_slice_in_dim(near_pairs, first_slot, group_size, 0)
        targets = chosen[:, 0]
        sources = chosen[:, 1]
        active = (first_slot + jnp.arange(group_size, dtype=jnp.int32) < near_count[0]).astype(
            jnp.float32
        )
        target_pos = positions[targets].reshape(group_size, 3, elems)
        source_pos = ext_pos[sources].reshape(group_size, 3, elems)
        source_disp = ext_disp[sources].reshape(group_size, 3, elems)
        contrib = kernel_block(target_pos, source_pos, source_disp) * active[:, None, None]
        return summed.at[targets].add(contrib.reshape(group_size, row_width))

    near_sum = lax.fori_loop(
        0, near_slots // group_size, near_step, jnp.zeros((clusters, row_width), jnp.float32)
    )
    disp_bf = displacement.astype(jnp.bfloat16)
    coeff = jnp.einsum("kf,kfr->kr", disp_bf, cluster_basis, preferred_element_type=jnp.float32)
    coeff_bf = coeff.astype(jnp.bfloat16)
    column = lax.all_gather(coeff_bf, "rows", axis=0, tiled=True)
    far_slots = far_pairs.shape[0]
    far_active = (jnp.arange(far_slots, dtype=jnp.int32) < far_count[0]).astype(jnp.float32)
    gathered = column[far_pairs[:, 1]]
    coupled = (
        jnp.einsum("prs,ps->pr", far_blocks, gathered, preferred_element_type=jnp.float32)
        * far_active[:, None]
    )
    row_clusters = clusters * lax.axis_size("cols")
    partial_sum = (
        jnp.zeros((row_clusters, coeff.shape[1]), jnp.float32).at[far_pairs[:, 0]].add(coupled)
    )
    whole = lax.psum(partial_sum.astype(jnp.bfloat16), "cols").astype(jnp.float32)
    owned = lax.dynamic_slice_in_dim(whole, lax.axis_index("cols") * clusters, clusters, 0)
    owned_bf = owned.astype(jnp.bfloat16)
    far_part = jnp.einsum("kfr,kr->kf", cluster_basis, owned_bf, preferred_element_type=jnp.float32)
    traction = near_sum + far_part
    disp3 = displacement.reshape(clusters, 3, elems)
    separation = jnp.sqrt(1.0 + jnp.sum(disp3 * disp3, axis=1))
    softened = 1.0 - jnp.exp(-(separation - 1.0) / softening)
    intact_float = intact.astype(jnp.float32)
    damage = intact_float * softened + (1.0 - intact_float)
    holding = ((1.0 - damage) * stiffness)[:, None, :] * disp3
    net_traction = traction - holding.reshape(clusters, row_width)
    return (net_traction, damage)


def solution(mesh):
    in_specs = (
        P(("rows", "cols"), None),
        P(("rows", "cols"), None),
        P(("rows", "cols"), None, None),
        P(("rows", "cols"), None),
        P(("rows", "cols")),
        P(("rows", "cols"), None),
        P(("rows", "cols")),
        P(("rows", "cols"), None, None),
        P(("rows", "cols"), None),
        P(("rows", "cols"), None),
    )
    out_specs = (P(("rows", "cols"), None), P(("rows", "cols"), None))
    return jax.shard_map(local, mesh=mesh, in_specs=in_specs, out_specs=out_specs, check_vma=False)
```

profile of v0, /device:TPU:8, one launch (start us, length us, event | category | flops | bytes accessed | tf_op | source)
XLA Modules:
  0.0 270.3 jit_solution(5717524596262092971)
XLA Ops:
  8.7 9.7 %collective-permute-start.1 = (f32[2,2,288]{2,1,0:T(2,128)}, f32[2,2,288]{2,1,0:T(2,128)}, u32[]{:S(2)}, u32[]{:S(2)}) collective-permute-start(f32[2,2,288]{2,1,0:T(2,128)} %get-tuple-element.156), channel_id=1, source_target_pairs={{1,0},{2,1},{3,2},{4,3},{5,4},{6,5},{7,6},{8,7},{9,8},{10,9},{11,1... | collective-permute-start | bytes 13832 | tf_op jit(solution)/shard_map/ppermute | solution.py:22
  22.8 29.2 %copy.15 = bf16[1024,64,64]{1,2,0:T(8,128)(2,1)} copy(bf16[1024,64,64]{0,2,1:T(8,128)(2,1)} %param.19) | data formatting | bytes 16777216 | tf_op args[7]
  53.2 17.2 %all_gather.3 = bf16[1024,64]{1,0:T(8,128)(2,1)S(1)} all-gather(bf16[64,64]{1,0:T(8,128)(2,1)S(1)} %convert_element_type.37), channel_id=1, replica_groups=mesh['rows'=16,'cols'=16] {'rows'}, dimensions={0}, use_global_device_ids=true | all-gather | bytes 139264 | tf_op jit(solution)/shard_map/all_gather | solution.py:80
  71.1 4.3 %gather_fusion.3 = bf16[1024,64]{1,0:T(8,128)(2,1)} fusion(bf16[1024,64]{1,0:T(8,128)(2,1)S(1)} %all_gather.3, s32[1024]{0:T(1024)S(1)} %broadcast_clamp_fusion), kind=kCustom, calls=%fused_computation.3 | custom fusion | bytes 266240 | tf_op jit(solution)/shard_map/gather | solution.py:83
  75.3 8.9 %fusion.8 = f32[1024,1,64]{2,1,0:T(1,128)} fusion(bf16[1024,64,64]{1,2,0:T(8,128)(2,1)} %copy.15, bf16[1024,64,1]{1,0,2:T(8,128)(2,1)} %bitcast.40), kind=kOutput, calls=%fused_computation.27 | convolution fusion | flops 8388608 | bytes 8781824 | tf_op jit(solution)/shard_map/prs,ps->pr/dot_general | solution.py:85
  84.2 7.8 %scatter_custom_fusion.1 = f32[1024,64]{1,0:T(8,128)} fusion(s32[1024]{0:T(1024)S(1)} %bitcast.43, f32[1024,64]{1,0:T(8,128)} %bitcast.39, f32[1024]{0:T(1024)S(1)} %fusion.20, f32[]{:T(128)} %constant.75.clone.1), kind=kCustom, calls=%fused_computation.29 | custom fusion | flops 131072 | bytes 528388 | tf_op jit(solution)/shard_map/scatter-add | solution.py:90
  98.5 152.6 %while.13 = (s32[]{:T(128)}, f32[64,288]{1,0:T(8,128)}, s32[256,2]{0,1:T(2,128)S(1)}, f32[64,288]{1,0:T(8,128)S(1)}, f32[68,288]{1,0:T(8,128)S(1)}, /*index=5*/f...) while((s32[]{:T(128)}, f32[64,288]{1,0:T(8,128)}, ...), condition=%wide.region_6.0_spmd, body=%wide.region_0.0_spmd.sunk | while | flops 9752870 | bytes 10787303 | solution.py:74
  104.8 2.9 %fusion.30 = (f32[32,96,96]{2,1,0:T(8,128)S(1)}, f32[32,96,96]{2,1,0:T(8,128)S(1)}) fusion(f32[32,3,96]{2,1,0:T(4,128)} %mul.270, f32[32,3,96]{2,1,0:T(4,128)S(1)} %sub.113, f32[32,3,96]{2,1,0:T(4,128)} %sub.114), kind=kLoop, calls=%fused_computation.10.clone.1 | loop fusion | flops 3833856 | bytes 2469888 | tf_op jit(solution)/shard_map/while/body/eval_jaxpr/reduce_sum | solution.py:32
  110.3 3.3 %fusion.31 = f32[32,3,96]{2,1,0:T(4,128)S(1)} fusion(f32[32,96,96]{2,1,0:T(8,128)S(1)} %get-tuple-element.217, f32[32,3,96]{2,1,0:T(4,128)S(1)} %sub.113, f32[32,3,96]{2,1,0:T(4,128)S(1)} %copy-done.2), kind=kLoop, calls=%fused_computation.11.clone.1 | loop fusion | flops 2644992 | bytes 1290240 | tf_op jit(solution)/shard_map/while/body/eval_jaxpr/reduce_sum | solution.py:34
  115.0 2.6 scatter_custom_fusion.7
  123.8 2.9 %fusion.30 = (f32[32,96,96]{2,1,0:T(8,128)S(1)}, f32[32,96,96]{2,1,0:T(8,128)S(1)}) fusion(f32[32,3,96]{2,1,0:T(4,128)} %mul.270, f32[32,3,96]{2,1,0:T(4,128)S(1)} %sub.113, f32[32,3,96]{2,1,0:T(4,128)} %sub.114), kind=kLoop, calls=%fused_computation.10.clone.1 | loop fusion | flops 3833856 | bytes 2469888 | tf_op jit(solution)/shard_map/while/body/eval_jaxpr/reduce_sum | solution.py:32
  129.4 3.3 %fusion.31 = f32[32,3,96]{2,1,0:T(4,128)S(1)} fusion(f32[32,96,96]{2,1,0:T(8,128)S(1)} %get-tuple-element.217, f32[32,3,96]{2,1,0:T(4,128)S(1)} %sub.113, f32[32,3,96]{2,1,0:T(4,128)S(1)} %copy-done.2), kind=kLoop, calls=%fused_computation.11.clone.1 | loop fusion | flops 2644992 | bytes 1290240 | tf_op jit(solution)/shard_map/while/body/eval_jaxpr/reduce_sum | solution.py:34
  134.1 2.6 scatter_custom_fusion.7
  142.9 2.9 %fusion.30 = (f32[32,96,96]{2,1,0:T(8,128)S(1)}, f32[32,96,96]{2,1,0:T(8,128)S(1)}) fusion(f32[32,3,96]{2,1,0:T(4,128)} %mul.270, f32[32,3,96]{2,1,0:T(4,128)S(1)} %sub.113, f32[32,3,96]{2,1,0:T(4,128)} %sub.114), kind=kLoop, calls=%fused_computation.10.clone.1 | loop fusion | flops 3833856 | bytes 2469888 | tf_op jit(solution)/shard_map/while/body/eval_jaxpr/reduce_sum | solution.py:32
  148.4 3.3 %fusion.31 = f32[32,3,96]{2,1,0:T(4,128)S(1)} fusion(f32[32,96,96]{2,1,0:T(8,128)S(1)} %get-tuple-element.217, f32[32,3,96]{2,1,0:T(4,128)S(1)} %sub.113, f32[32,3,96]{2,1,0:T(4,128)S(1)} %copy-done.2), kind=kLoop, calls=%fused_computation.11.clone.1 | loop fusion | flops 2644992 | bytes 1290240 | tf_op jit(solution)/shard_map/while/body/eval_jaxpr/reduce_sum | solution.py:34
  153.2 2.6 scatter_custom_fusion.7
  162.0 2.9 %fusion.30 = (f32[32,96,96]{2,1,0:T(8,128)S(1)}, f32[32,96,96]{2,1,0:T(8,128)S(1)}) fusion(f32[32,3,96]{2,1,0:T(4,128)} %mul.270, f32[32,3,96]{2,1,0:T(4,128)S(1)} %sub.113, f32[32,3,96]{2,1,0:T(4,128)} %sub.114), kind=kLoop, calls=%fused_computation.10.clone.1 | loop fusion | flops 3833856 | bytes 2469888 | tf_op jit(solution)/shard_map/while/body/eval_jaxpr/reduce_sum | solution.py:32
  167.5 3.3 %fusion.31 = f32[32,3,96]{2,1,0:T(4,128)S(1)} fusion(f32[32,96,96]{2,1,0:T(8,128)S(1)} %get-tuple-element.217, f32[32,3,96]{2,1,0:T(4,128)S(1)} %sub.113, f32[32,3,96]{2,1,0:T(4,128)S(1)} %copy-done.2), kind=kLoop, calls=%fused_computation.11.clone.1 | loop fusion | flops 2644992 | bytes 1290240 | tf_op jit(solution)/shard_map/while/body/eval_jaxpr/reduce_sum | solution.py:34
  172.2 2.6 scatter_custom_fusion.7
  181.1 2.9 %fusion.30 = (f32[32,96,96]{2,1,0:T(8,128)S(1)}, f32[32,96,96]{2,1,0:T(8,128)S(1)}) fusion(f32[32,3,96]{2,1,0:T(4,128)} %mul.270, f32[32,3,96]{2,1,0:T(4,128)S(1)} %sub.113, f32[32,3,96]{2,1,0:T(4,128)} %sub.114), kind=kLoop, calls=%fused_computation.10.clone.1 | loop fusion | flops 3833856 | bytes 2469888 | tf_op jit(solution)/shard_map/while/body/eval_jaxpr/reduce_sum | solution.py:32
  186.6 3.3 %fusion.31 = f32[32,3,96]{2,1,0:T(4,128)S(1)} fusion(f32[32,96,96]{2,1,0:T(8,128)S(1)} %get-tuple-element.217, f32[32,3,96]{2,1,0:T(4,128)S(1)} %sub.113, f32[32,3,96]{2,1,0:T(4,128)S(1)} %copy-done.2), kind=kLoop, calls=%fused_computation.11.clone.1 | loop fusion | flops 2644992 | bytes 1290240 | tf_op jit(solution)/shard_map/while/body/eval_jaxpr/reduce_sum | solution.py:34
  191.3 2.6 scatter_custom_fusion.7
  200.2 2.9 %fusion.30 = (f32[32,96,96]{2,1,0:T(8,128)S(1)}, f32[32,96,96]{2,1,0:T(8,128)S(1)}) fusion(f32[32,3,96]{2,1,0:T(4,128)} %mul.270, f32[32,3,96]{2,1,0:T(4,128)S(1)} %sub.113, f32[32,3,96]{2,1,0:T(4,128)} %sub.114), kind=kLoop, calls=%fused_computation.10.clone.1 | loop fusion | flops 3833856 | bytes 2469888 | tf_op jit(solution)/shard_map/while/body/eval_jaxpr/reduce_sum | solution.py:32
  205.7 3.3 %fusion.31 = f32[32,3,96]{2,1,0:T(4,128)S(1)} fusion(f32[32,96,96]{2,1,0:T(8,128)S(1)} %get-tuple-element.217, f32[32,3,96]{2,1,0:T(4,128)S(1)} %sub.113, f32[32,3,96]{2,1,0:T(4,128)S(1)} %copy-done.2), kind=kLoop, calls=%fused_computation.11.clone.1 | loop fusion | flops 2644992 | bytes 1290240 | tf_op jit(solution)/shard_map/while/body/eval_jaxpr/reduce_sum | solution.py:34
  210.4 2.6 scatter_custom_fusion.7
  219.2 2.9 %fusion.30 = (f32[32,96,96]{2,1,0:T(8,128)S(1)}, f32[32,96,96]{2,1,0:T(8,128)S(1)}) fusion(f32[32,3,96]{2,1,0:T(4,128)} %mul.270, f32[32,3,96]{2,1,0:T(4,128)S(1)} %sub.113, f32[32,3,96]{2,1,0:T(4,128)} %sub.114), kind=kLoop, calls=%fused_computation.10.clone.1 | loop fusion | flops 3833856 | bytes 2469888 | tf_op jit(solution)/shard_map/while/body/eval_jaxpr/reduce_sum | solution.py:32
  224.8 3.3 %fusion.31 = f32[32,3,96]{2,1,0:T(4,128)S(1)} fusion(f32[32,96,96]{2,1,0:T(8,128)S(1)} %get-tuple-element.217, f32[32,3,96]{2,1,0:T(4,128)S(1)} %sub.113, f32[32,3,96]{2,1,0:T(4,128)S(1)} %copy-done.2), kind=kLoop, calls=%fused_computation.11.clone.1 | loop fusion | flops 2644992 | bytes 1290240 | tf_op jit(solution)/shard_map/while/body/eval_jaxpr/reduce_sum | solution.py:34
  229.5 2.6 scatter_custom_fusion.7
  238.3 2.9 %fusion.30 = (f32[32,96,96]{2,1,0:T(8,128)S(1)}, f32[32,96,96]{2,1,0:T(8,128)S(1)}) fusion(f32[32,3,96]{2,1,0:T(4,128)} %mul.270, f32[32,3,96]{2,1,0:T(4,128)S(1)} %sub.113, f32[32,3,96]{2,1,0:T(4,128)} %sub.114), kind=kLoop, calls=%fused_computation.10.clone.1 | loop fusion | flops 3833856 | bytes 2469888 | tf_op jit(solution)/shard_map/while/body/eval_jaxpr/reduce_sum | solution.py:32
  243.8 3.3 %fusion.31 = f32[32,3,96]{2,1,0:T(4,128)S(1)} fusion(f32[32,96,96]{2,1,0:T(8,128)S(1)} %get-tuple-element.217, f32[32,3,96]{2,1,0:T(4,128)S(1)} %sub.113, f32[32,3,96]{2,1,0:T(4,128)S(1)} %copy-done.2), kind=kLoop, calls=%fused_computation.11.clone.1 | loop fusion | flops 2644992 | bytes 1290240 | tf_op jit(solution)/shard_map/while/body/eval_jaxpr/reduce_sum | solution.py:34
  248.6 2.6 scatter_custom_fusion.7
  251.2 10.2 %all-reduce.2.cloned.1.call-done = bf16[1024,64]{1,0:T(8,128)(2,1)} async-done(((bf16[1024,64]{1,0:T(8,128)(2,1)}), bf16[1024,64]{1,0:T(8,128)(2,1)}) %all-reduce.2.cloned.1.call-update) | async-done | bytes 131088 | tf_op jit(solution)/shard_map/psum | solution.py:92
  (182 shorter events, 96.9 us)
Async XLA Ops:
  7.2 44.8 %copy-start = (bf16[64,288,64]{1,2,0:T(8,128)(2,1)S(1)}, bf16[64,288,64]{1,2,0:T(8,128)(2,1)}, u32[]{:S(2)}) copy-start(bf16[64,288,64]{1,2,0:T(8,128)(2,1)} %param.14) | copy-start | bytes 7077892
  7.2 254.2 %all-reduce.2.cloned.1.call-start = ((), (), s32[]{:S(2)}) async-start(), calls=%async_computation | async-start | bytes 524288 | tf_op jit(solution)/shard_map/psum | solution.py:92
  8.7 88.4 %collective-permute-start.1 = (f32[2,2,288]{2,1,0:T(2,128)}, f32[2,2,288]{2,1,0:T(2,128)}, u32[]{:S(2)}, u32[]{:S(2)}) collective-permute-start(f32[2,2,288]{2,1,0:T(2,128)} %get-tuple-element.156), channel_id=1, source_target_pairs={{1,0},{2,1},{3,2},{4,3},{5,4},{6,5},{7,6},{8,7},{9,8},{10,9},{11,1... | collective-permute-start | bytes 13832 | tf_op jit(solution)/shard_map/ppermute | solution.py:22
  18.5 78.6 %collective-permute-start = (f32[2,2,288]{2,1,0:T(2,128)S(1)}, f32[2,2,288]{2,1,0:T(2,128)}, u32[]{:S(2)}, u32[]{:S(2)}) collective-permute-start(f32[2,2,288]{2,1,0:T(2,128)S(1)} %get-tuple-element.155), channel_id=1, source_target_pairs={{0,1},{1,2},{2,3},{3,4},{4,5},{5,6},{6,7},{7,8},{8,9},{9,10},{10,1... | collective-permute-start | bytes 13832 | tf_op jit(solution)/shard_map/ppermute | solution.py:21
  84.2 12.9 %copy-start.1 = (f32[64,288]{1,0:T(8,128)S(1)}, f32[64,288]{1,0:T(8,128)}, u32[]{:S(2)}) copy-start(f32[64,288]{1,0:T(8,128)} %param.13) | copy-start | bytes 221188
  84.2 12.9 %copy-start.4 = (f32[64,288]{1,0:T(8,128)S(1)}, f32[64,288]{1,0:T(8,128)}, u32[]{:S(2)}) copy-start(f32[64,288]{1,0:T(8,128)} %param.12) | copy-start | bytes 221188
  84.2 14.3 %copy-start.8 = (s32[256,2]{0,1:T(2,128)S(1)}, s32[256,2]{0,1:T(2,128)}, u32[]{:S(2)}) copy-start(s32[256,2]{0,1:T(2,128)} %param.15) | copy-start | bytes 6148
  107.7 0.8 copy-start.3
  107.7 2.6 copy-start.2
  126.8 0.8 copy-start.3
  126.8 2.6 copy-start.2
  145.8 0.8 copy-start.3
  145.9 2.6 copy-start.2
  164.9 0.8 copy-start.3
  164.9 2.6 copy-start.2
  184.0 0.8 copy-start.3
  184.0 2.6 copy-start.2
  203.1 0.8 copy-start.3
  203.1 2.6 copy-start.2
  222.2 0.8 copy-start.3
  222.2 2.6 copy-start.2
  241.2 0.8 copy-start.3
  241.3 2.6 copy-start.2
  251.2 11.6 %copy-start.5 = (f32[64,288]{1,0:T(8,128)S(1)}, f32[64,288]{1,0:T(8,128)}, u32[]{:S(2)}) copy-start(f32[64,288]{1,0:T(8,128)} %param.12) | copy-start | bytes 221188
  251.2 11.6 %copy-start.6 = (f32[64,288]{1,0:T(8,128)S(1)}, f32[64,288]{1,0:T(8,128)}, u32[]{:S(2)}) copy-start(f32[64,288]{1,0:T(8,128)} %mul.200) | copy-start | bytes 221188
  251.2 11.6 %copy-start.7 = (f32[64,288]{1,0:T(8,128)S(1)}, f32[64,288]{1,0:T(8,128)}, u32[]{:S(2)}) copy-start(f32[64,288]{1,0:T(8,128)} %get-tuple-element.126) | copy-start | bytes 221188
Sparse Core Ops, SparseCore 0:
  93.9 167.4 all-reduce.1
where the time goes:
time: 274 us; the launch traced here: 270 us
  other arithmetic  111 us (41%)
  local copies, waits for them, and re-layouts  94.2 us (34%)
  blocking collectives  17.2 us (6%)
  between operations  14.8 us (5%)
  starting transfers between devices  11.7 us (4%)
  matrix products  10.7 us (4%)
  waiting for transfers between devices  10.2 us (4%)
    unnamed x15, local copies, waits for them, and re-layouts  29.2 us
    reduce_sum x8, other arithmetic, kernel_block(): jnp.sum(offsets * (along * inverse / distance)[:, None, :, :], axis=3)  26.6 us
    reduce_sum x8, other arithmetic, kernel_block(): along = jnp.sum(offsets * source_disp[:, :, None, :], axis=1)  23.3 us
    scatter-add x8, other arithmetic, near_step(): return summed.at[targets].add(contrib.reshape(group_size, row_width))  20.8 us
    sub x16, local copies, waits for them, and re-layouts, kernel_block(): offsets = target_pos[:, :, :, None] - source_pos[:, :, None, :]  19.3 us
    all_gather x1, blocking collectives, local(): column = lax.all_gather(coeff_bf, 'rows', axis=0, tiled=True)  17.2 us
    reduce_sum x8, other arithmetic, kernel_block(): jnp.sum(inverse[:, None, :, :] * source_disp[:, :, None, :], axis=3)  13.9 us
    psum x1, waiting for transfers between devices, local(): lax.psum(partial_sum.astype(jnp.bfloat16), 'cols').astype(jnp.float32)  10.2 us
  transfers between devices with their start and end apart: 3, of which 1 were waited for; matrix products, arithmetic and copies ran while one was open for 77% of the time, Pallas kernels for 0%

commit v1 on v0

v1 whole, which is shorter than its diff:
```python
import functools

import jax
import jax.numpy as jnp
from jax import lax
from jax.experimental import pallas as pl
from jax.experimental.pallas import tpu as pltpu
from jax.sharding import PartitionSpec as P

MESH = pl.DeviceIdType.MESH
ELEMS = 96
RANK = 64
OWN = 64
WIDTH = 3 * ELEMS
LANES = 128
GROUPS = OWN // 4
core_square = 0.25
softening = 1.5

FIRST = (1, 6)
SECOND = (6, 11)
THIRD = (11, 15)


def mega(
    n_rows,
    n_cols,
    coeff,
    disp,
    pos,
    near_pairs,
    near_count,
    far_pairs,
    far_count,
    far_hbm,
    near_out,
    owned_out,
    ext_disp,
    ext_pos,
    turned,
    wide,
    targets,
    weights,
    near_sum,
    far_blocks,
    column,
    coupled,
    split,
    partial,
    arrived,
    far_sem,
    halo_send,
    halo_recv,
    gather_send,
    gather_recv,
    scatter_send,
    scatter_recv,
):
    f32, bf16 = jnp.float32, jnp.bfloat16
    i, j = lax.axis_index("rows"), lax.axis_index("cols")
    me = i * n_cols + j
    devices = n_rows * n_cols
    after = (me + 1) % devices
    before = (me + devices - 1) % devices
    next_id = (after // n_cols, after % n_cols)
    last_id = (before // n_cols, before % n_cols)
    row_peers = [((i + d) % n_rows, j) for d in range(1, n_rows)]
    col_peers = [(i, (j + d) % n_cols) for d in range(1, n_cols)]

    far_copy = pltpu.make_async_copy(far_hbm, far_blocks, far_sem)
    far_copy.start()
    barrier = pltpu.get_barrier_semaphore()
    peers = row_peers + col_peers + [next_id, last_id]
    for peer in peers:
        pl.semaphore_signal(barrier, inc=1, device_id=peer, device_id_type=MESH)

    ext_disp[0:OWN, :] = disp[...]
    ext_pos[0:OWN, :] = pos[...]

    def turn(rows):
        for c in range(3):
            lanes = slice(c * ELEMS, (c + 1) * ELEMS)
            turned[c, :, 0:rows] = ext_pos[0:rows, lanes].T
            turned[3 + c, :, 0:rows] = ext_disp[0:rows, lanes].T

    turn(OWN)
    for c in range(3):
        wide[:, 0:ELEMS] = pos[:, c * ELEMS : (c + 1) * ELEMS]
        a0, a1, a2, a3 = [wide[pl.ds(m, GROUPS, stride=4), :][:, :ELEMS] for m in range(4)]
        targets[c, 0] = jnp.concatenate([a0, a1[:, :32]], axis=1)
        targets[c, 1] = jnp.concatenate([a1[:, 32:], a2[:, :64]], axis=1)
        targets[c, 2] = jnp.concatenate([a2[:, 64:], a3], axis=1)

    slots = near_pairs.shape[1]
    near_target = near_pairs[0:1, :]
    near_source = near_pairs[1:2, :]
    group = near_target // 4
    live = lax.broadcasted_iota(jnp.int32, (1, slots), 1) < near_count[0]
    row = jnp.where(live, group * 8 + near_source - group * 4, -1)
    place = near_target - group * 4
    row_is = (lax.broadcasted_iota(jnp.int32, (8 * GROUPS, slots), 0) == row).astype(f32)
    lane_is = (lax.broadcasted_iota(jnp.int32, (4 * ELEMS, slots), 0) // ELEMS == place).astype(f32)
    for v in range(3):
        weights[v] = lax.dot_general(
            row_is.astype(bf16),
            lane_is[v * LANES : (v + 1) * LANES].astype(bf16),
            (((1,), (1,)), ((), ())),
            preferred_element_type=f32,
        )

    def near_group(g, _):
        shift = (130 - 4 * g) % LANES
        xs = [[jnp.broadcast_to(targets[c, v, pl.ds(g, 1), :], (8, LANES)) for c in range(3)] for v in range(3)]

        def step(part, totals):
            totals = [list(t) for t in totals]
            first = pl.multiple_of(part * 8, 8)
            tiles = [pltpu.roll(turned[q, pl.ds(first, 8), :], shift, axis=1) for q in range(6)]
            for s in range(8):
                y = [jnp.broadcast_to(tiles[c][:, s : s + 1], (8, LANES)) for c in range(3)]
                u = [jnp.broadcast_to(tiles[3 + c][:, s : s + 1], (8, LANES)) for c in range(3)]
                for v in range(3):
                    if not v <= s <= v + 5:
                        continue
                    r = [xs[v][c] - y[c] for c in range(3)]
                    q = (r[0] * r[0] + r[1] * r[1]) + (r[2] * r[2] + core_square)
                    inverse = lax.rsqrt(q)
                    square = inverse * inverse
                    count = jnp.broadcast_to(weights[v, pl.ds(8 * g + s, 1), :], (8, LANES))
                    cube = (square * inverse) * count
                    along = (r[0] * u[0] + r[1] * u[1] + r[2] * u[2]) * (3.0 * square)
                    for c in range(3):
                        totals[v][c] = totals[v][c] + cube * (u[c] - along * r[c])
            return totals

        zero = [[jnp.zeros((8, LANES), f32) for _ in range(3)] for _ in range(3)]
        totals = lax.fori_loop(0, ELEMS // 8, step, zero)
        for v in range(3):
            for c in range(3):
                near_sum[c, v, pl.ds(g, 1), :] = jnp.sum(totals[v][c], axis=0, keepdims=True)
        return 0

    lax.fori_loop(*FIRST, near_group, 0)
    pl.semaphore_wait(barrier, len(peers))

    def remote(src, dst, send, recv, peer):
        return pltpu.make_async_remote_copy(
            src_ref=src, dst_ref=dst, send_sem=send, recv_sem=recv, device_id=peer, device_id_type=MESH
        )

    mine = column.at[pl.ds(pl.multiple_of(i * OWN, OWN), OWN), :]
    gathers = [
        remote(coeff, mine, gather_send.at[d], gather_recv.at[d], peer) for d, peer in enumerate(row_peers)
    ]
    halos = []
    for n, (src, dst) in enumerate(((disp, ext_disp), (pos, ext_pos))):
        halos.append(remote(src.at[pl.ds(OWN - 8, 8), :], dst.at[pl.ds(120, 8), :], halo_send.at[n], halo_recv.at[n], next_id))
        halos.append(remote(src.at[pl.ds(0, 8), :], dst.at[pl.ds(OWN, 8), :], halo_send.at[2 + n], halo_recv.at[2 + n], last_id))
    for copy in gathers + halos:
        copy.start()
    column[pl.ds(pl.multiple_of(i * OWN, OWN), OWN), :] = coeff[...]

    lax.fori_loop(*SECOND, near_group, 0)

    for copy in gathers:
        copy.wait()
    far_copy.wait()
    column_turned = column[...].astype(f32).T.astype(bf16)
    far_slots = far_pairs.shape[1]
    sources = n_rows * OWN

    def couple(block, _):
        first = pl.multiple_of(block * LANES, LANES)
        source = far_pairs[1:2, pl.ds(first, LANES)]
        alive = lax.broadcasted_iota(jnp.int32, (1, LANES), 1) + first < far_count[0]
        source = jnp.where(alive, source, -1)
        chosen = (lax.broadcasted_iota(jnp.int32, (sources, LANES), 0) == source).astype(f32).astype(bf16)
        gathered = jnp.dot(column_turned, chosen, preferred_element_type=f32)

        def ranks(part, _):
            top = pl.multiple_of(part * 8, 8)
            blocks = far_blocks[pl.ds(top, 8), :, pl.ds(first, LANES)].astype(f32)
            coupled[pl.ds(top, 8), pl.ds(first, LANES)] = jnp.sum(blocks * gathered[None], axis=1)
            return 0

        return lax.fori_loop(0, RANK // 8, ranks, 0)

    lax.fori_loop(0, far_slots // LANES, couple, 0)
    whole = coupled[...]
    high = whole.astype(bf16)
    split[0:RANK, :] = high
    split[RANK : 2 * RANK, :] = (whole - high.astype(f32)).astype(bf16)

    def collect(block, _):
        first = pl.multiple_of(block * LANES, LANES)
        chosen = (lax.broadcasted_iota(jnp.int32, (LANES, far_slots), 0) + first == far_pairs[0:1, :]).astype(f32)
        both = lax.dot_general(
            chosen.astype(bf16), split[...], (((1,), (1,)), ((), ())), preferred_element_type=f32
        )
        partial[pl.ds(first, LANES), :] = (both[:, :RANK] + both[:, RANK:]).astype(bf16)
        return 0

    lax.fori_loop(0, n_cols * OWN // LANES, collect, 0)

    for copy in halos:
        copy.wait()

    here = pl.ds(pl.multiple_of(j * OWN, OWN), OWN)
    scatters = []
    for d, peer in enumerate(col_peers):
        block = partial.at[pl.ds(pl.multiple_of(peer[1] * OWN, OWN), OWN), :]
        scatters.append(remote(block, arrived.at[here, :], scatter_send.at[d], scatter_recv.at[d], peer))
    for copy in scatters:
        copy.start()
    arrived[here, :] = partial[here, :]

    ext_disp[OWN : OWN + 8, :] = jnp.where(me == devices - 1, 0.0, ext_disp[OWN : OWN + 8, :])
    ext_disp[120:128, :] = jnp.where(me == 0, 0.0, ext_disp[120:128, :])
    turn(2 * OWN)
    lax.fori_loop(*THIRD, near_group, 0)
    near_group(0, 0)
    near_group(GROUPS - 1, 0)

    quarters = [[], [], [], []]
    for c in range(3):
        v0, v1, v2 = [near_sum[c, v] for v in range(3)]
        quarters[0].append(v0[:, :96])
        quarters[1].append(jnp.concatenate([v0[:, 96:], v1[:, :64]], axis=1))
        quarters[2].append(jnp.concatenate([v1[:, 64:], v2[:, :32]], axis=1))
        quarters[3].append(v2[:, 32:])
    for m in range(4):
        near_out[m] = jnp.concatenate(quarters[m], axis=1)

    for copy in scatters:
        copy.wait()
    owned = arrived[0:OWN, :].astype(f32)
    for n in range(1, n_cols):
        owned = owned + arrived[n * OWN : (n + 1) * OWN, :].astype(f32)
    owned_out[...] = owned.astype(bf16)


def local(
    displacement,
    positions,
    cluster_basis,
    near_pairs,
    near_count,
    far_pairs,
    far_count,
    far_blocks,
    intact,
    stiffness,
):
    n_rows, n_cols = lax.axis_size("rows"), lax.axis_size("cols")
    f32, bf16 = jnp.float32, jnp.bfloat16
    disp_bf = displacement.astype(bf16)
    coeff = jnp.einsum("kf,kfr->kr", disp_bf, cluster_basis, preferred_element_type=f32).astype(bf16)
    far_slots = far_pairs.shape[0]
    vmem = pl.BlockSpec(memory_space=pltpu.VMEM)
    smem = pl.BlockSpec(memory_space=pltpu.SMEM)
    near, owned = pl.pallas_call(
        functools.partial(mega, n_rows, n_cols),
        out_shape=(
            jax.ShapeDtypeStruct((4, GROUPS, WIDTH), f32),
            jax.ShapeDtypeStruct((OWN, RANK), bf16),
        ),
        in_specs=[vmem, vmem, vmem, vmem, smem, vmem, smem, pl.BlockSpec(memory_space=pl.ANY)],
        out_specs=(vmem, vmem),
        scratch_shapes=[
            pltpu.VMEM((2 * OWN, WIDTH), f32),
            pltpu.VMEM((2 * OWN, WIDTH), f32),
            pltpu.VMEM((6, ELEMS, LANES), f32),
            pltpu.VMEM((OWN, LANES), f32),
            pltpu.VMEM((3, 3, GROUPS, LANES), f32),
            pltpu.VMEM((3, 8 * GROUPS, LANES), f32),
            pltpu.VMEM((3, 3, GROUPS, LANES), f32),
            pltpu.VMEM((RANK, RANK, far_slots), bf16),
            pltpu.VMEM((n_rows * OWN, RANK), bf16),
            pltpu.VMEM((RANK, far_slots), f32),
            pltpu.VMEM((2 * RANK, far_slots), bf16),
            pltpu.VMEM((n_cols * OWN, RANK), bf16),
            pltpu.VMEM((n_cols * OWN, RANK), bf16),
            pltpu.SemaphoreType.DMA,
            pltpu.SemaphoreType.DMA((4,)),
            pltpu.SemaphoreType.DMA((4,)),
            pltpu.SemaphoreType.DMA((n_rows - 1,)),
            pltpu.SemaphoreType.DMA((n_rows - 1,)),
            pltpu.SemaphoreType.DMA((n_cols - 1,)),
            pltpu.SemaphoreType.DMA((n_cols - 1,)),
        ],
        compiler_params=pltpu.CompilerParams(
            collective_id=0, has_side_effects=True, vmem_limit_bytes=40 * 1024 * 1024
        ),
        name="traction",
    )(
        coeff,
        displacement,
        positions,
        near_pairs.T,
        near_count,
        far_pairs.T,
        far_count,
        jnp.transpose(far_blocks, (1, 2, 0)),
    )
    near_sum = jnp.swapaxes(near, 0, 1).reshape(OWN, WIDTH)
    far_part = jnp.einsum("kfr,kr->kf", cluster_basis, owned, preferred_element_type=f32)
    traction = near_sum + far_part
    disp3 = displacement.reshape(OWN, 3, ELEMS)
    separation = jnp.sqrt(1.0 + jnp.sum(disp3 * disp3, axis=1))
    softened = 1.0 - jnp.exp(-(separation - 1.0) / softening)
    intact_float = intact.astype(f32)
    damage = intact_float * softened + (1.0 - intact_float)
    holding = ((1.0 - damage) * stiffness)[:, None, :] * disp3
    net_traction = traction - holding.reshape(OWN, WIDTH)
    return (net_traction, damage)


def solution(mesh):
    both = ("rows", "cols")
    in_specs = (
        P(both, None),
        P(both, None),
        P(both, None, None),
        P(both, None),
        P(both),
        P(both, None),
        P(both),
        P(both, None, None),
        P(both, None),
        P(both, None),
    )
    out_specs = (P(both, None), P(both, None))
    return jax.shard_map(local, mesh=mesh, in_specs=in_specs, out_specs=out_specs, check_vma=False)
```

time: 274 us -> 70 us (0.26)
  the two profiles are of different devices: /device:TPU:8 before, /device:TPU:1 now
where the time goes in v1:
time: 70 us; the launch traced here: 69.7 us
  Pallas kernels  54.9 us (78%)
  local copies, waits for them, and re-layouts  6.15 us (9%)
  other arithmetic  3.93 us (6%)
  matrix products  2.62 us (4%)
  between operations  2.07 us (3%)
    pallas_call x1, Pallas kernels, local(): pl.pallas_call(functools.partial(mega, n_rows, n_cols), out_shape=(jax.Sh...  54.9 us
    unnamed x16, local copies, waits for them, and re-layouts  3.66 us
    dot_general x1, matrix products, local(): jnp.einsum('kf,kfr->kr', disp_bf, cluster_basis, preferred_element_type=f32)  1.97 us
    convert_element_type x1, other arithmetic, local(): disp_bf = displacement.astype(bf16)  1.76 us
    mul x1, other arithmetic, local(): holding = ((1.0 - damage) * stiffness)[:, None, :] * disp3  1.42 us

profile of v1, /device:TPU:1, one launch (start us, length us, event | category | flops | bytes accessed | tf_op | source)
XLA Modules:
  0.0 69.7 jit_solution(3341194907819874827)
XLA Ops:
  0.6 0.0 copy-start
  0.6 0.0 copy-start.2
  0.7 0.0 copy-start.5
  0.7 0.0 copy-start.4
  0.7 0.0 copy-start.3
  0.7 1.8 %convert_bitcast_fusion = (bf16[64,288,1]{1,0,2:T(8,128)(2,1)}, f32[64,288]{1,0:T(8,128)}) fusion(f32[64,288]{1,0:T(8,128)} %disp.1), kind=kLoop, calls=%fused_computation.4 | loop fusion | flops 36864 | bytes 184320 | tf_op jit(solution)/shard_map/convert_element_type | solution.py:256
  2.4 1.0 %mul.24 = f32[64,3,96]{2,1,0:T(4,128)S(1)} reshape(f32[64,288]{1,0:T(8,128)} %get-tuple-element.9) | data formatting | bytes 147456 | tf_op jit(solution)/shard_map/mul | solution.py:309
  3.5 0.1 reduce_sum.9
  3.6 1.4 %subtract_multiply_fusion = (f32[64,96]{1,0:T(8,128)S(1)}, f32[64,96]{1,0:T(8,128)}) fusion(f32[64,96]{1,0:T(8,128)} %param.19, f32[64,96]{1,0:T(8,128)S(1)} %reduce_sum.9, s32[64,96]{1,0:T(8,128)} %param.18), kind=kLoop, calls=%fused_computation.7 | loop fusion | flops 67584 | bytes 122880 | tf_op jit(solution)/shard_map/mul | solution.py:313
  5.0 0.7 %mul.28 = f32[64,288]{1,0:T(8,128)} reshape(f32[64,3,96]{2,1,0:T(4,128)S(1)} %mul.27) | data formatting | bytes 147456 | tf_op jit(solution)/shard_map/mul | solution.py:313
  5.7 0.0 copy-done
  5.7 2.0 %fusion.1 = f32[64,1,64]{2,1,0:T(1,128)S(1)} fusion(bf16[64,288,64]{1,2,0:T(8,128)(2,1)S(1)} %copy-done, bf16[64,288,1]{1,0,2:T(8,128)(2,1)} %get-tuple-element.8), kind=kOutput, calls=%fused_computation.2 | convolution fusion | flops 2359296 | bytes 2412544 | tf_op jit(solution)/shard_map/kf,kfr->kr/dot_general | solution.py:257
  9.0 0.0 copy-done.2
  9.1 0.0 copy-done.5
  9.1 0.0 copy-done.4
  9.1 0.0 copy-done.3
  9.1 0.0 copy-start.1
  9.1 3.4 %copy-done.1 = bf16[1024,64,64]{0,2,1:T(8,128)(2,1)S(1)} copy-done((bf16[1024,64,64]{0,2,1:T(8,128)(2,1)S(1)}, bf16[1024,64,64]{0,2,1:T(8,128)(2,1)}, u32[]{:S(2)}) %copy-start.1) | copy-done | bytes 8388632
  12.5 54.9 %traction.1 = (f32[4,16,288]{2,1,0:T(8,128)S(1)}, bf16[64,64]{1,0:T(8,128)(2,1)S(1)}) custom-call(bf16[64,64]{1,0:T(8,128)(2,1)S(1)} %convert_element_type.10.coeff, f32[64,288]{1,0:T(8,128)S(1)} %copy-done.2, f32[64,288]{1,0:T(8,128)S(1)} %copy-done.3, s32[2,256]{1,0:T(2,128)S(1)} %bitcast.19, s32[1]{0:T(128)S(6)} %copy.22.near_count, ...), custom_call_target="tpu_custom_call" | custom-call | tf_op jit(solution)/shard_map/traction/pallas_call | solution.py:261
  67.4 0.0 copy-start.6
  67.4 0.7 reshape.12
  68.1 0.0 copy-start.7
  68.1 0.6 fusion.3
  68.8 0.0 copy-done.6
  68.8 0.3 copy-done.7
  69.0 0.7 fusion
  (3 shorter events, 0.1 us)
Async XLA Ops:
  0.6 5.1 %copy-start = (bf16[64,288,64]{1,2,0:T(8,128)(2,1)S(1)}, bf16[64,288,64]{1,2,0:T(8,128)(2,1)}, u32[]{:S(2)}) copy-start(bf16[64,288,64]{1,2,0:T(8,128)(2,1)} %param.12) | copy-start | bytes 7077892
  0.6 8.4 %copy-start.2 = (f32[64,288]{1,0:T(8,128)S(1)}, f32[64,288]{1,0:T(8,128)}, u32[]{:S(2)}) copy-start(f32[64,288]{1,0:T(8,128)} %disp.1) | copy-start | bytes 221188
  0.7 8.4 %copy-start.5 = (s32[256,2]{0,1:T(2,128)S(1)}, s32[256,2]{0,1:T(2,128)}, u32[]{:S(2)}) copy-start(s32[256,2]{0,1:T(2,128)} %param.13) | copy-start | bytes 6148
  0.7 8.4 %copy-start.4 = (s32[1024,2]{0,1:T(2,128)S(1)}, s32[1024,2]{0,1:T(2,128)}, u32[]{:S(2)}) copy-start(s32[1024,2]{0,1:T(2,128)} %param.15) | copy-start | bytes 24580
  0.7 8.4 %copy-start.3 = (f32[64,288]{1,0:T(8,128)S(1)}, f32[64,288]{1,0:T(8,128)}, u32[]{:S(2)}) copy-start(f32[64,288]{1,0:T(8,128)} %pos.1) | copy-start | bytes 221188
  9.1 3.4 %copy-start.1 = (bf16[1024,64,64]{0,2,1:T(8,128)(2,1)S(1)}, bf16[1024,64,64]{0,2,1:T(8,128)(2,1)}, u32[]{:S(2)}) copy-start(bf16[1024,64,64]{0,2,1:T(8,128)(2,1)} %param.17) | copy-start | bytes 25165828
  67.4 1.4 %copy-start.6 = (f32[64,288]{1,0:T(8,128)S(1)}, f32[64,288]{1,0:T(8,128)}, u32[]{:S(2)}) copy-start(f32[64,288]{1,0:T(8,128)} %mul.28) | copy-start | bytes 221188
  68.1 0.9 %copy-start.7 = (f32[64,288]{1,0:T(8,128)S(1)}, f32[64,288]{1,0:T(8,128)}, u32[]{:S(2)}) copy-start(f32[64,288]{1,0:T(8,128)} %reshape.12) | copy-start | bytes 221188

commit v2 on v1

--- a/solution.py
+++ b/solution.py
@@ -19,21 +19,24 @@
 
 FIRST = (1, 6)
 SECOND = (6, 11)
-THIRD = (11, 15)
+THIRD = (11, 16)
 
 
 def mega(
     n_rows,
     n_cols,
-    coeff,
     disp,
     pos,
     near_pairs,
     near_count,
     far_pairs,
     far_count,
+    intact,
+    stiffness,
+    basis_hbm,
     far_hbm,
-    near_out,
+    base_out,
+    damage_out,
     owned_out,
     ext_disp,
     ext_pos,
@@ -41,13 +44,17 @@
     wide,
     targets,
     weights,
+    spread,
     near_sum,
+    near_rows,
+    basis,
     far_blocks,
     column,
     coupled,
     split,
     partial,
     arrived,
+    basis_sem,
     far_sem,
     halo_send,
     halo_recv,
@@ -67,6 +74,8 @@
     row_peers = [((i + d) % n_rows, j) for d in range(1, n_rows)]
     col_peers = [(i, (j + d) % n_cols) for d in range(1, n_cols)]
 
+    basis_copy = pltpu.make_async_copy(basis_hbm, basis, basis_sem)
+    basis_copy.start()
     far_copy = pltpu.make_async_copy(far_hbm, far_blocks, far_sem)
     far_copy.start()
     barrier = pltpu.get_barrier_semaphore()
@@ -108,39 +117,69 @@
             preferred_element_type=f32,
         )
 
-    def near_group(g, _):
+    def fill(buffer, g, part):
         shift = (130 - 4 * g) % LANES
+        first = pl.multiple_of(part * 8, 8)
+        for q in range(6):
+            tile = pltpu.roll(turned[q, pl.ds(first, 8), :], shift, axis=1)
+            for s in range(8):
+                buffer[6 * s + q] = jnp.broadcast_to(tile[:, s : s + 1], (8, LANES))
+
+    def interact(buffer, g, totals):
+        totals = [list(t) for t in totals]
         xs = [[jnp.broadcast_to(targets[c, v, pl.ds(g, 1), :], (8, LANES)) for c in range(3)] for v in range(3)]
-
-        def step(part, totals):
-            totals = [list(t) for t in totals]
-            first = pl.multiple_of(part * 8, 8)
-            tiles = [pltpu.roll(turned[q, pl.ds(first, 8), :], shift, axis=1) for q in range(6)]
-            for s in range(8):
-                y = [jnp.broadcast_to(tiles[c][:, s : s + 1], (8, LANES)) for c in range(3)]
-                u = [jnp.broadcast_to(tiles[3 + c][:, s : s + 1], (8, LANES)) for c in range(3)]
-                for v in range(3):
-                    if not v <= s <= v + 5:
-                        continue
-                    r = [xs[v][c] - y[c] for c in range(3)]
-                    q = (r[0] * r[0] + r[1] * r[1]) + (r[2] * r[2] + core_square)
-                    inverse = lax.rsqrt(q)
-                    square = inverse * inverse
-                    count = jnp.broadcast_to(weights[v, pl.ds(8 * g + s, 1), :], (8, LANES))
-                    cube = (square * inverse) * count
-                    along = (r[0] * u[0] + r[1] * u[1] + r[2] * u[2]) * (3.0 * square)
-                    for c in range(3):
-                        totals[v][c] = totals[v][c] + cube * (u[c] - along * r[c])
-            return totals
-
-        zero = [[jnp.zeros((8, LANES), f32) for _ in range(3)] for _ in range(3)]
-        totals = lax.fori_loop(0, ELEMS // 8, step, zero)
-        for v in range(3):
-            for c in range(3):
-                near_sum[c, v, pl.ds(g, 1), :] = jnp.sum(totals[v][c], axis=0, keepdims=True)
-        return 0
-
-    lax.fori_loop(*FIRST, near_group, 0)
+        for s in range(8):
+            y = [buffer[6 * s + c] for c in range(3)]
+            u = [buffer[6 * s + 3 + c] for c in range(3)]
+            for v in range(3):
+                if not v <= s <= v + 5:
+                    continue
+                r = [xs[v][c] - y[c] for c in range(3)]
+                q = (r[0] * r[0] + r[1] * r[1]) + (r[2] * r[2] + core_square)
+                inverse = lax.rsqrt(q)
+                square = inverse * inverse
+                count = jnp.broadcast_to(weights[v, pl.ds(8 * g + s, 1), :], (8, LANES))
+                cube = (square * inverse) * count
+                along = (r[0] * u[0] + r[1] * u[1] + r[2] * u[2]) * (3.0 * square)
+                for c in range(3):
+                    totals[v][c] = totals[v][c] + cube * (u[c] - along * r[c])
+        return totals
+
+    def near_groups(first, last):
+        fill(spread, first, 0)
+
+        def one(g, _):
+            def one_part(p, totals):
+                totals = interact(spread, g, totals)
+                wrap = p == ELEMS // 8 - 1
+                fill(spread, jnp.where(wrap, g + 1, g), jnp.where(wrap, 0, p + 1))
+                return totals
+
+            zero = [[jnp.zeros((8, LANES), f32) for _ in range(3)] for _ in range(3)]
+            totals = lax.fori_loop(0, ELEMS // 8, one_part, zero)
+            for v in range(3):
+                for c in range(3):
+                    near_sum[c, v, pl.ds(g, 1), :] = jnp.sum(totals[v][c], axis=0, keepdims=True)
+            return 0
+
+        lax.fori_loop(first, last, one, 0)
+
+    basis_copy.wait()
+
+    def project(block, coeff):
+        top = pl.multiple_of(block * 8, 8)
+        rows = disp[pl.ds(top, 8), :].astype(bf16).astype(f32)
+        lane = lax.broadcasted_iota(jnp.int32, (RANK, OWN), 1)
+        for n in range(8):
+            product = basis[top + n].astype(f32) * rows[n : n + 1, :]
+            coeff = jnp.where(lane == top + n, jnp.sum(product, axis=1, keepdims=True), coeff)
+        return coeff
+
+    coeff = lax.fori_loop(0, OWN // 8, project, jnp.zeros((RANK, OWN), f32))
+    own_rows = pl.ds(pl.multiple_of(i * OWN, OWN), OWN)
+    column[own_rows, :] = coeff.astype(bf16)
+
+    near_groups(*FIRST)
     pl.semaphore_wait(barrier, len(peers))
 
     def remote(src, dst, send, recv, peer):
@@ -148,9 +187,9 @@
             src_ref=src, dst_ref=dst, send_sem=send, recv_sem=recv, device_id=peer, device_id_type=MESH
         )
 
-    mine = column.at[pl.ds(pl.multiple_of(i * OWN, OWN), OWN), :]
+    mine = column.at[own_rows, :]
     gathers = [
-        remote(coeff, mine, gather_send.at[d], gather_recv.at[d], peer) for d, peer in enumerate(row_peers)
+        remote(mine, mine, gather_send.at[d], gather_recv.at[d], peer) for d, peer in enumerate(row_peers)
     ]
     halos = []
     for n, (src, dst) in enumerate(((disp, ext_disp), (pos, ext_pos))):
@@ -158,14 +197,13 @@
         halos.append(remote(src.at[pl.ds(0, 8), :], dst.at[pl.ds(OWN, 8), :], halo_send.at[2 + n], halo_recv.at[2 + n], last_id))
     for copy in gathers + halos:
         copy.start()
-    column[pl.ds(pl.multiple_of(i * OWN, OWN), OWN), :] = coeff[...]
-
-    lax.fori_loop(*SECOND, near_group, 0)
+
+    near_groups(*SECOND)
 
     for copy in gathers:
         copy.wait()
     far_copy.wait()
-    column_turned = column[...].astype(f32).T.astype(bf16)
+    column_turned = jnp.concatenate([column[n * OWN : (n + 1) * OWN, :] for n in range(n_rows)], axis=1)
     far_slots = far_pairs.shape[1]
     sources = n_rows * OWN
 
@@ -217,19 +255,26 @@
     ext_disp[OWN : OWN + 8, :] = jnp.where(me == devices - 1, 0.0, ext_disp[OWN : OWN + 8, :])
     ext_disp[120:128, :] = jnp.where(me == 0, 0.0, ext_disp[120:128, :])
     turn(2 * OWN)
-    lax.fori_loop(*THIRD, near_group, 0)
-    near_group(0, 0)
-    near_group(GROUPS - 1, 0)
-
-    quarters = [[], [], [], []]
+    near_groups(*THIRD)
+    near_groups(0, 1)
+
+    parts = []
     for c in range(3):
         v0, v1, v2 = [near_sum[c, v] for v in range(3)]
-        quarters[0].append(v0[:, :96])
-        quarters[1].append(jnp.concatenate([v0[:, 96:], v1[:, :64]], axis=1))
-        quarters[2].append(jnp.concatenate([v1[:, 64:], v2[:, :32]], axis=1))
-        quarters[3].append(v2[:, 32:])
-    for m in range(4):
-        near_out[m] = jnp.concatenate(quarters[m], axis=1)
+        pad = jnp.zeros((GROUPS, LANES - ELEMS), f32)
+        near_rows[pl.ds(0, GROUPS, stride=4), :] = v0
+        near_rows[pl.ds(1, GROUPS, stride=4), :] = jnp.concatenate([v0[:, 96:], v1[:, :64], pad], axis=1)
+        near_rows[pl.ds(2, GROUPS, stride=4), :] = jnp.concatenate([v1[:, 64:], v2[:, :32], pad], axis=1)
+        near_rows[pl.ds(3, GROUPS, stride=4), :] = jnp.concatenate([v2[:, 32:], pad], axis=1)
+        parts.append(near_rows[:, :ELEMS])
+    u = [disp[:, c * ELEMS : (c + 1) * ELEMS] for c in range(3)]
+    separation = jnp.sqrt(1.0 + (u[0] * u[0] + u[1] * u[1] + u[2] * u[2]))
+    softened = 1.0 - jnp.exp(-(separation - 1.0) / softening)
+    whole_element = intact[...].astype(f32)
+    damage = whole_element * softened + (1.0 - whole_element)
+    damage_out[...] = damage
+    held = (1.0 - damage) * stiffness[...]
+    base_out[...] = jnp.concatenate([parts[c] - held * u[c] for c in range(3)], axis=1)
 
     for copy in scatters:
         copy.wait()
@@ -253,19 +298,19 @@
 ):
     n_rows, n_cols = lax.axis_size("rows"), lax.axis_size("cols")
     f32, bf16 = jnp.float32, jnp.bfloat16
-    disp_bf = displacement.astype(bf16)
-    coeff = jnp.einsum("kf,kfr->kr", disp_bf, cluster_basis, preferred_element_type=f32).astype(bf16)
     far_slots = far_pairs.shape[0]
     vmem = pl.BlockSpec(memory_space=pltpu.VMEM)
     smem = pl.BlockSpec(memory_space=pltpu.SMEM)
-    near, owned = pl.pallas_call(
+    hbm = pl.BlockSpec(memory_space=pl.ANY)
+    base, damage, owned = pl.pallas_call(
         functools.partial(mega, n_rows, n_cols),
         out_shape=(
-            jax.ShapeDtypeStruct((4, GROUPS, WIDTH), f32),
+            jax.ShapeDtypeStruct((OWN, WIDTH), f32),
+            jax.ShapeDtypeStruct((OWN, ELEMS), f32),
             jax.ShapeDtypeStruct((OWN, RANK), bf16),
         ),
-        in_specs=[vmem, vmem, vmem, vmem, smem, vmem, smem, pl.BlockSpec(memory_space=pl.ANY)],
-        out_specs=(vmem, vmem),
+        in_specs=[vmem, vmem, vmem, smem, vmem, smem, vmem, vmem, hbm, hbm],
+        out_specs=(vmem, vmem, vmem),
         scratch_shapes=[
             pltpu.VMEM((2 * OWN, WIDTH), f32),
             pltpu.VMEM((2 * OWN, WIDTH), f32),
@@ -273,13 +318,17 @@
             pltpu.VMEM((OWN, LANES), f32),
             pltpu.VMEM((3, 3, GROUPS, LANES), f32),
             pltpu.VMEM((3, 8 * GROUPS, LANES), f32),
+            pltpu.VMEM((48, 8, LANES), f32),
             pltpu.VMEM((3, 3, GROUPS, LANES), f32),
+            pltpu.VMEM((OWN, LANES), f32),
+            pltpu.VMEM((OWN, RANK, WIDTH), bf16),
             pltpu.VMEM((RANK, RANK, far_slots), bf16),
             pltpu.VMEM((n_rows * OWN, RANK), bf16),
             pltpu.VMEM((RANK, far_slots), f32),
             pltpu.VMEM((2 * RANK, far_slots), bf16),
             pltpu.VMEM((n_cols * OWN, RANK), bf16),
             pltpu.VMEM((n_cols * OWN, RANK), bf16),
+            pltpu.SemaphoreType.DMA,
             pltpu.SemaphoreType.DMA,
             pltpu.SemaphoreType.DMA((4,)),
             pltpu.SemaphoreType.DMA((4,)),
@@ -293,26 +342,19 @@
         ),
         name="traction",
     )(
-        coeff,
         displacement,
         positions,
         near_pairs.T,
         near_count,
         far_pairs.T,
         far_count,
+        intact,
+        stiffness,
+        jnp.transpose(cluster_basis, (0, 2, 1)),
         jnp.transpose(far_blocks, (1, 2, 0)),
     )
-    near_sum = jnp.swapaxes(near, 0, 1).reshape(OWN, WIDTH)
     far_part = jnp.einsum("kfr,kr->kf", cluster_basis, owned, preferred_element_type=f32)
-    traction = near_sum + far_part
-    disp3 = displacement.reshape(OWN, 3, ELEMS)
-    separation = jnp.sqrt(1.0 + jnp.sum(disp3 * disp3, axis=1))
-    softened = 1.0 - jnp.exp(-(separation - 1.0) / softening)
-    intact_float = intact.astype(f32)
-    damage = intact_float * softened + (1.0 - intact_float)
-    holding = ((1.0 - damage) * stiffness)[:, None, :] * disp3
-    net_traction = traction - holding.reshape(OWN, WIDTH)
-    return (net_traction, damage)
+    return (base + far_part, damage)
 
 
 def solution(mesh):

time: 70 us -> 70.9 us (1.013)
  local copies, waits for them, and re-layouts: 6.15 us -> 10.6 us
  other arithmetic: 3.93 us -> 0.66 us
  matrix products: 2.62 us -> 0.65 us
  Pallas kernels: 54.9 us -> 56.6 us
    unnamed x16 -> x17, local copies, waits for them, and re-layouts: 3.66 us -> 10.6 us
    dot_general x1 -> x0, matrix products: 1.97 us -> none  [local(): jnp.einsum('kf,kfr->kr', disp_bf, cluster_basis, preferred_element_type=f32)]
    mul x3 -> x0, local copies, waits for them, and re-layouts: 1.78 us -> none  [the longest x1 1.01 us: local(): separation = jnp.sqrt(1.0 + jnp.sum(disp3 * disp3, axis=1))]
    convert_element_type x2 -> x0, other arithmetic: 1.77 us -> none  [the longest x1 1.76 us: local(): disp_bf = displacement.astype(bf16)]
    pallas_call x1, Pallas kernels: 54.9 us -> 56.6 us  [local(): pl.pallas_call(functools.partial(mega, n_rows, n_cols), out_shape=(jax.Sh...]
    mul x1 -> x0, other arithmetic: 1.42 us -> none  [local(): holding = ((1.0 - damage) * stiffness)[:, None, :] * disp3]
where the time goes in v2:
time: 70.9 us; the launch traced here: 70.5 us
  Pallas kernels  56.6 us (80%)
  local copies, waits for them, and re-layouts  10.6 us (15%)
  between operations  1.95 us (3%)
    pallas_call x1, Pallas kernels, local(): pl.pallas_call(functools.partial(mega, n_rows, n_cols), out_shape=(jax.Sh...  56.6 us
    unnamed x17, local copies, waits for them, and re-layouts  10.6 us

profile of v2, /device:TPU:1, one launch (start us, length us, event | category | flops | bytes accessed | tf_op | source)
XLA Modules:
  0.0 70.5 jit_solution(2619095683658886206)
XLA Ops:
  1.9 0.0 copy-start
  1.9 1.9 %copy-done = bf16[64,288,64]{1,2,0:T(8,128)(2,1)S(1)} copy-done((bf16[64,288,64]{1,2,0:T(8,128)(2,1)S(1)}, bf16[64,288,64]{1,2,0:T(8,128)(2,1)}, u32[]{:S(2)}) %copy-start) | copy-done | bytes 2359320
  3.8 0.0 copy-start.1
  3.8 3.4 %copy-done.1 = bf16[1024,64,64]{0,2,1:T(8,128)(2,1)S(1)} copy-done((bf16[1024,64,64]{0,2,1:T(8,128)(2,1)S(1)}, bf16[1024,64,64]{0,2,1:T(8,128)(2,1)}, u32[]{:S(2)}) %copy-start.1) | copy-done | bytes 8388632
  7.2 0.0 copy-start.2
  7.2 0.9 %copy-done.2 = f32[64,288]{1,0:T(8,128)S(1)} copy-done((f32[64,288]{1,0:T(8,128)S(1)}, f32[64,288]{1,0:T(8,128)}, u32[]{:S(2)}) %copy-start.2) | copy-done | bytes 73752
  8.1 0.0 copy-start.3
  8.1 0.9 %copy-done.3 = f32[64,288]{1,0:T(8,128)S(1)} copy-done((f32[64,288]{1,0:T(8,128)S(1)}, f32[64,288]{1,0:T(8,128)}, u32[]{:S(2)}) %copy-start.3) | copy-done | bytes 73752
  9.0 0.0 copy-start.4
  9.0 0.8 %copy-done.4 = s32[64,96]{1,0:T(8,128)S(1)} copy-done((s32[64,96]{1,0:T(8,128)S(1)}, s32[64,96]{1,0:T(8,128)}, u32[]{:S(2)}) %copy-start.4) | copy-done | bytes 24600
  9.7 0.0 copy-start.5
  9.7 0.8 %copy-done.5 = f32[64,96]{1,0:T(8,128)S(1)} copy-done((f32[64,96]{1,0:T(8,128)S(1)}, f32[64,96]{1,0:T(8,128)}, u32[]{:S(2)}) %copy-start.5) | copy-done | bytes 24600
  10.5 0.0 copy-start.6
  10.5 0.7 copy-done.6
  11.2 0.0 copy-start.7
  11.2 0.7 copy-done.7
  11.9 56.6 %traction.1 = (f32[64,288]{1,0:T(8,128)S(1)}, f32[64,96]{1,0:T(8,128)S(1)}, bf16[64,64]{1,0:T(8,128)(2,1)S(1)}) custom-call(f32[64,288]{1,0:T(8,128)S(1)} %copy-done.2, f32[64,288]{1,0:T(8,128)S(1)} %copy-done.3, s32[2,256]{1,0:T(2,128)S(1)} %bitcast.12, s32[1]{0:T(128)S(6)} %copy.18.near_count, s32[2,1024]{1,0:T(2,128)S(1)} %bitcast.11, ...), custom_call_target="tpu_custom_call" | custom-call | tf_op jit(solution)/shard_map/traction/pallas_call | solution.py:305
  68.5 0.6 fusion
  69.2 0.7 bitcast_add_fusion
  69.8 0.6 copy.20
Async XLA Ops:
  1.9 1.9 %copy-start = (bf16[64,288,64]{1,2,0:T(8,128)(2,1)S(1)}, bf16[64,288,64]{1,2,0:T(8,128)(2,1)}, u32[]{:S(2)}) copy-start(bf16[64,288,64]{1,2,0:T(8,128)(2,1)} %param.12) | copy-start | bytes 7077892
  3.8 3.4 %copy-start.1 = (bf16[1024,64,64]{0,2,1:T(8,128)(2,1)S(1)}, bf16[1024,64,64]{0,2,1:T(8,128)(2,1)}, u32[]{:S(2)}) copy-start(bf16[1024,64,64]{0,2,1:T(8,128)(2,1)} %param.17) | copy-start | bytes 25165828
  7.2 0.9 %copy-start.2 = (f32[64,288]{1,0:T(8,128)S(1)}, f32[64,288]{1,0:T(8,128)}, u32[]{:S(2)}) copy-start(f32[64,288]{1,0:T(8,128)} %disp.1) | copy-start | bytes 221188
  8.1 0.9 %copy-start.3 = (f32[64,288]{1,0:T(8,128)S(1)}, f32[64,288]{1,0:T(8,128)}, u32[]{:S(2)}) copy-start(f32[64,288]{1,0:T(8,128)} %pos.1) | copy-start | bytes 221188
  9.0 0.8 %copy-start.4 = (s32[64,96]{1,0:T(8,128)S(1)}, s32[64,96]{1,0:T(8,128)}, u32[]{:S(2)}) copy-start(s32[64,96]{1,0:T(8,128)} %intact.1) | copy-start | bytes 73732
  9.7 0.8 %copy-start.5 = (f32[64,96]{1,0:T(8,128)S(1)}, f32[64,96]{1,0:T(8,128)}, u32[]{:S(2)}) copy-start(f32[64,96]{1,0:T(8,128)} %stiffness.1) | copy-start | bytes 73732
  10.5 0.7 copy-start.6
  11.2 0.7 copy-start.7

commit v3 on v2

v3 whole, which is shorter than its diff:
```python
import functools

import jax
import jax.numpy as jnp
from jax import lax
from jax.experimental import pallas as pl
from jax.experimental.pallas import tpu as pltpu
from jax.sharding import PartitionSpec as P

MESH = pl.DeviceIdType.MESH
ELEMS = 96
RANK = 64
OWN = 64
WIDTH = 3 * ELEMS
LANES = 128
GROUPS = OWN // 4
core_square = 0.25
softening = 1.5

PIECES = ((0, 0), (0, 1), (1, 0), (1, 1), (0, 2), (2, 0))
SEEN = (range(0, 4), range(0, 5), range(1, 6), range(2, 6))
FIRST = (1, 6)
SECOND = (6, 11)
THIRD = (11, 16)


def mega(
    n_rows,
    n_cols,
    near_count,
    far_count,
    disp_hbm,
    pos_hbm,
    near_pairs_hbm,
    far_pairs_hbm,
    intact_hbm,
    stiffness_hbm,
    basis_hbm,
    far_hbm,
    base_out,
    damage_out,
    owned_out,
    ext_disp,
    ext_pos,
    near_pairs,
    far_pairs,
    intact,
    stiffness,
    wide,
    centred,
    left,
    right_q,
    right_s,
    disp_rows,
    pos_rows,
    weights,
    near_rows,
    basis,
    far_blocks,
    column,
    coupled,
    split,
    partial,
    arrived,
    local_sem,
    halo_send,
    halo_recv,
    gather_send,
    gather_recv,
    scatter_send,
    scatter_recv,
):
    f32, bf16 = jnp.float32, jnp.bfloat16
    i, j = lax.axis_index("rows"), lax.axis_index("cols")
    me = i * n_cols + j
    devices = n_rows * n_cols
    after = (me + 1) % devices
    before = (me + devices - 1) % devices
    next_id = (after // n_cols, after % n_cols)
    last_id = (before // n_cols, before % n_cols)
    row_peers = [((i + d) % n_rows, j) for d in range(1, n_rows)]
    col_peers = [(i, (j + d) % n_cols) for d in range(1, n_cols)]

    own = pl.ds(0, OWN)
    loads = [
        pltpu.make_async_copy(src, dst, local_sem.at[n])
        for n, (src, dst) in enumerate(
            (
                (disp_hbm, ext_disp.at[own, :]),
                (pos_hbm, ext_pos.at[own, :]),
                (near_pairs_hbm, near_pairs),
                (basis_hbm, basis),
                (far_pairs_hbm, far_pairs),
                (intact_hbm, intact),
                (stiffness_hbm, stiffness),
                (far_hbm, far_blocks),
            )
        )
    ]
    for copy in loads:
        copy.start()
    barrier = pltpu.get_barrier_semaphore()
    peers = row_peers + col_peers + [next_id, last_id]
    for peer in peers:
        pl.semaphore_signal(barrier, inc=1, device_id=peer, device_id_type=MESH)

    for copy in loads[:3]:
        copy.wait()

    def lanes_of(c):
        return slice(c * ELEMS, (c + 1) * ELEMS)

    def thirds(x):
        high = x.astype(bf16).astype(f32)
        middle = (x - high).astype(bf16).astype(f32)
        return high, middle, (x - high) - middle

    def square_sum(x):
        return x[0] * x[0] + x[1] * x[1] + x[2] * x[2]

    gap = jnp.zeros((GROUPS, LANES - ELEMS), f32)
    one = jnp.ones((GROUPS, LANES), f32)
    none = jnp.zeros((GROUPS, LANES), f32)

    def rows_of(n, stride):
        return pl.ds(n, GROUPS, stride=stride)

    def widen(n, ext, c, halo):
        wide[n, 2 : OWN + 2, 0:ELEMS] = ext[0:OWN, lanes_of(c)]
        if halo:
            wide[n, 0:2, 0:ELEMS] = ext[126:128, lanes_of(c)]
            wide[n, OWN + 2 : OWN + 4, 0:ELEMS] = ext[OWN : OWN + 2, lanes_of(c)]

    def build(halo):
        for c in range(3):
            widen(c, ext_pos, c, halo)
            widen(3 + c, ext_disp, c, halo)
        centre = []
        for c in range(3):
            inner = wide[c, rows_of(3, 4), :][:, :ELEMS] + wide[c, rows_of(4, 4), :][:, :ELEMS]
            centre.append(jnp.sum(inner, axis=1, keepdims=True) * (0.5 / ELEMS))
        if not halo:
            for m in range(4):
                x = [wide[c, rows_of(2 + m, 4), :][:, :ELEMS] - centre[c] for c in range(3)]
                x = [jnp.concatenate([v, gap], axis=1) for v in x]
                parts = [thirds(v) for v in x]
                norm = thirds(square_sum(x))
                for c in range(3):
                    centred[c, rows_of(m, 4), :] = x[c]
                    for n, (a, _) in enumerate(PIECES):
                        left[rows_of(24 * m + 3 * n + c, 96), :] = parts[c][a]
                for n in range(3):
                    left[rows_of(24 * m + 18 + n, 96), :] = one
                    left[rows_of(24 * m + 21 + n, 96), :] = norm[n]

        def packed(n, half):
            a0, a1, a2, a3 = [wide[n, rows_of(4 * half + m, 4), :][:, :ELEMS] for m in range(4)]
            return (
                jnp.concatenate([a0, a1[:, :32]], axis=1),
                jnp.concatenate([a1[:, 32:], a2[:, :64]], axis=1),
                jnp.concatenate([a2[:, 64:], a3], axis=1),
            )

        for half in range(2):
            sources = [packed(n, half) for n in range(6)]
            for v in range(3):
                w = 3 * half + v
                y = [sources[c][v] - centre[c] for c in range(3)]
                u = [sources[3 + c][v] for c in range(3)]
                y_parts = [thirds(value) for value in y]
                u_parts = [thirds(value) for value in u]
                norm = thirds(square_sum(y) + core_square)
                inner = thirds(y[0] * u[0] + y[1] * u[1] + y[2] * u[2])
                for c in range(3):
                    for n, (_, b) in enumerate(PIECES):
                        right_q[w, rows_of(3 * n + c, 24), :] = -2.0 * y_parts[c][b]
                        right_s[w, rows_of(3 * n + c, 24), :] = u_parts[c][b]
                    disp_rows[w, rows_of(c, 8), :] = u[c]
                    pos_rows[w, rows_of(c, 8), :] = 3.0 * y[c]
                for n in range(3):
                    right_q[w, rows_of(18 + n, 24), :] = norm[n]
                    right_s[w, rows_of(18 + n, 24), :] = -inner[n]
                    right_q[w, rows_of(21 + n, 24), :] = one
                    right_s[w, rows_of(21 + n, 24), :] = none
                for n in range(3, 8):
                    disp_rows[w, rows_of(n, 8), :] = none
                    pos_rows[w, rows_of(n, 8), :] = 3.0 * one if n == 3 else none

    wide[...] = jnp.zeros_like(wide)
    build(False)

    slots = near_pairs.shape[1]
    near_target = near_pairs[0:1, :]
    live = lax.broadcasted_iota(jnp.int32, (1, slots), 1) < near_count[0]
    place = near_pairs[1:2, :] - near_target // 4 * 4
    row_is = lax.broadcasted_iota(jnp.int32, (OWN, slots), 0) == jnp.where(live, near_target, -1)
    lane_is = lax.broadcasted_iota(jnp.int32, (8 * ELEMS, slots), 0) // ELEMS == place
    row_is = row_is.astype(f32).astype(bf16)
    for w in range(6):
        weights[w] = lax.dot_general(
            row_is,
            lane_is[w * LANES : (w + 1) * LANES].astype(f32).astype(bf16),
            (((1,), (1,)), ((), ())),
            preferred_element_type=f32,
        )

    def halves(x):
        high = x.astype(bf16)
        return high, (x - high.astype(f32)).astype(bf16)

    def three_rows(x):
        return jnp.concatenate(thirds(x) + (jnp.zeros_like(x),), axis=0).astype(bf16)

    def near_groups(first, last):
        def near_group(g, _):
            top = pl.multiple_of(g * 24, 8)
            right = [
                jnp.concatenate([right_q[w, pl.ds(top, 24), :], right_s[w, pl.ds(top, 24), :]], axis=1).astype(bf16)
                for w in range(6)
            ]
            eight = pl.ds(pl.multiple_of(g * 8, 8), 8)
            for m in range(4):
                mine = left[pl.ds(pl.multiple_of(g * 96 + 24 * m, 8), 24), :]
                mine = mine.T[:ELEMS].astype(bf16)
                total = jnp.zeros((ELEMS, 32), f32)
                for w in SEEN[m]:
                    both = jnp.dot(mine, right[w], preferred_element_type=f32)
                    inverse = lax.rsqrt(jnp.maximum(both[:, :LANES], core_square))
                    square = inverse * inverse
                    cube = square * inverse
                    pull = both[:, LANES:] * square * cube
                    values = jnp.concatenate(halves(cube) + halves(pull), axis=1)
                    count = jnp.broadcast_to(weights[w, pl.ds(4 * g + m, 1), :], (8, LANES))
                    u_rows = three_rows(disp_rows[w, eight, :] * count)
                    y_rows = three_rows(pos_rows[w, eight, :] * count)
                    total = total + lax.dot_general(
                        values,
                        jnp.concatenate([u_rows, u_rows, y_rows, y_rows], axis=1),
                        (((1,), (1,)), ((), ())),
                        preferred_element_type=f32,
                    )
                total = total.T
                total = total[0:8] + total[8:16] + total[16:24]
                for c in range(3):
                    row = pl.ds(4 * g + m, 1)
                    near_rows[c, row, 0:ELEMS] = total[c : c + 1] - centred[c, row, 0:ELEMS] * total[3:4]
            return 0

        lax.fori_loop(first, last, near_group, 0)

    loads[3].wait()

    def project(block, coeff):
        top = pl.multiple_of(block * 8, 8)
        rows = ext_disp[pl.ds(top, 8), :].astype(bf16).astype(f32)
        lane = lax.broadcasted_iota(jnp.int32, (RANK, OWN), 1)
        for n in range(8):
            product = basis[top + n].astype(f32) * rows[n : n + 1, :]
            coeff = jnp.where(lane == top + n, jnp.sum(product, axis=1, keepdims=True), coeff)
        return coeff

    coeff = lax.fori_loop(0, OWN // 8, project, jnp.zeros((RANK, OWN), f32))
    own_rows = pl.ds(pl.multiple_of(i * OWN, OWN), OWN)
    column[own_rows, :] = coeff.astype(bf16)

    near_groups(*FIRST)
    pl.semaphore_wait(barrier, len(peers))

    def remote(src, dst, send, recv, peer):
        return pltpu.make_async_remote_copy(
            src_ref=src, dst_ref=dst, send_sem=send, recv_sem=recv, device_id=peer, device_id_type=MESH
        )

    mine = column.at[own_rows, :]
    gathers = [
        remote(mine, mine, gather_send.at[d], gather_recv.at[d], peer) for d, peer in enumerate(row_peers)
    ]
    halos = []
    for n, (src, dst) in enumerate(((disp_hbm, ext_disp), (pos_hbm, ext_pos))):
        halos.append(remote(src.at[pl.ds(OWN - 8, 8), :], dst.at[pl.ds(120, 8), :], halo_send.at[n], halo_recv.at[n], next_id))
        halos.append(remote(src.at[pl.ds(0, 8), :], dst.at[pl.ds(OWN, 8), :], halo_send.at[2 + n], halo_recv.at[2 + n], last_id))
    for copy in gathers + halos:
        copy.start()

    near_groups(*SECOND)

    for copy in gathers:
        copy.wait()
    for copy in loads[4:]:
        copy.wait()
    column_turned = jnp.concatenate([column[n * OWN : (n + 1) * OWN, :] for n in range(n_rows)], axis=1)
    far_slots = far_pairs.shape[1]
    sources = n_rows * OWN

    def couple(block, _):
        first = pl.multiple_of(block * LANES, LANES)
        source = far_pairs[1:2, pl.ds(first, LANES)]
        alive = lax.broadcasted_iota(jnp.int32, (1, LANES), 1) + first < far_count[0]
        source = jnp.where(alive, source, -1)
        chosen = (lax.broadcasted_iota(jnp.int32, (sources, LANES), 0) == source).astype(f32).astype(bf16)
        gathered = jnp.dot(column_turned, chosen, preferred_element_type=f32)

        def ranks(part, _):
            top = pl.multiple_of(part * 8, 8)
            blocks = far_blocks[pl.ds(top, 8), :, pl.ds(first, LANES)].astype(f32)
            coupled[pl.ds(top, 8), pl.ds(first, LANES)] = jnp.sum(blocks * gathered[None], axis=1)
            return 0

        return lax.fori_loop(0, RANK // 8, ranks, 0)

    lax.fori_loop(0, far_slots // LANES, couple, 0)
    whole = coupled[...]
    high = whole.astype(bf16)
    split[0:RANK, :] = high
    split[RANK : 2 * RANK, :] = (whole - high.astype(f32)).astype(bf16)

    def collect(block, _):
        first = pl.multiple_of(block * LANES, LANES)
        chosen = (lax.broadcasted_iota(jnp.int32, (LANES, far_slots), 0) + first == far_pairs[0:1, :]).astype(f32)
        both = lax.dot_general(
            chosen.astype(bf16), split[...], (((1,), (1,)), ((), ())), preferred_element_type=f32
        )
        partial[pl.ds(first, LANES), :] = (both[:, :RANK] + both[:, RANK:]).astype(bf16)
        return 0

    lax.fori_loop(0, n_cols * OWN // LANES, collect, 0)

    for copy in halos:
        copy.wait()

    here = pl.ds(pl.multiple_of(j * OWN, OWN), OWN)
    scatters = []
    for d, peer in enumerate(col_peers):
        block = partial.at[pl.ds(pl.multiple_of(peer[1] * OWN, OWN), OWN), :]
        scatters.append(remote(block, arrived.at[here, :], scatter_send.at[d], scatter_recv.at[d], peer))
    for copy in scatters:
        copy.start()
    arrived[here, :] = partial[here, :]

    ext_disp[OWN : OWN + 8, :] = jnp.where(me == devices - 1, 0.0, ext_disp[OWN : OWN + 8, :])
    ext_disp[120:128, :] = jnp.where(me == 0, 0.0, ext_disp[120:128, :])
    build(True)
    near_groups(*THIRD)
    near_groups(0, 1)

    parts = [near_rows[c, :, 0:ELEMS] for c in range(3)]
    u = [ext_disp[0:OWN, lanes_of(c)] for c in range(3)]
    separation = jnp.sqrt(1.0 + (u[0] * u[0] + u[1] * u[1] + u[2] * u[2]))
    softened = 1.0 - jnp.exp(-(separation - 1.0) / softening)
    whole_element = intact[...].astype(f32)
    damage = whole_element * softened + (1.0 - whole_element)
    damage_out[...] = damage
    held = (1.0 - damage) * stiffness[...]
    base_out[...] = jnp.concatenate([parts[c] - held * u[c] for c in range(3)], axis=1)

    for copy in scatters:
        copy.wait()
    owned = arrived[0:OWN, :].astype(f32)
    for n in range(1, n_cols):
        owned = owned + arrived[n * OWN : (n + 1) * OWN, :].astype(f32)
    owned_out[...] = owned.astype(bf16)


def local(
    displacement,
    positions,
    cluster_basis,
    near_pairs,
    near_count,
    far_pairs,
    far_count,
    far_blocks,
    intact,
    stiffness,
):
    n_rows, n_cols = lax.axis_size("rows"), lax.axis_size("cols")
    f32, bf16 = jnp.float32, jnp.bfloat16
    far_slots = far_pairs.shape[0]
    vmem = pl.BlockSpec(memory_space=pltpu.VMEM)
    smem = pl.BlockSpec(memory_space=pltpu.SMEM)
    hbm = pl.BlockSpec(memory_space=pltpu.HBM)
    base, damage, owned = pl.pallas_call(
        functools.partial(mega, n_rows, n_cols),
        out_shape=(
            jax.ShapeDtypeStruct((OWN, WIDTH), f32),
            jax.ShapeDtypeStruct((OWN, ELEMS), f32),
            jax.ShapeDtypeStruct((OWN, RANK), bf16),
        ),
        in_specs=[smem, smem] + [hbm] * 8,
        out_specs=(vmem, vmem, vmem),
        scratch_shapes=[
            pltpu.VMEM((2 * OWN, WIDTH), f32),
            pltpu.VMEM((2 * OWN, WIDTH), f32),
            pltpu.VMEM((2, near_pairs.shape[0]), jnp.int32),
            pltpu.VMEM((2, far_slots), jnp.int32),
            pltpu.VMEM((OWN, ELEMS), jnp.int32),
            pltpu.VMEM((OWN, ELEMS), f32),
            pltpu.VMEM((6, OWN + 8, LANES), f32),
            pltpu.VMEM((3, OWN, LANES), f32),
            pltpu.VMEM((24 * OWN, LANES), f32),
            pltpu.VMEM((6, 24 * GROUPS, LANES), f32),
            pltpu.VMEM((6, 24 * GROUPS, LANES), f32),
            pltpu.VMEM((6, 8 * GROUPS, LANES), f32),
            pltpu.VMEM((6, 8 * GROUPS, LANES), f32),
            pltpu.VMEM((6, OWN, LANES), f32),
            pltpu.VMEM((3, OWN, LANES), f32),
            pltpu.VMEM((OWN, RANK, WIDTH), bf16),
            pltpu.VMEM((RANK, RANK, far_slots), bf16),
            pltpu.VMEM((n_rows * OWN, RANK), bf16),
            pltpu.VMEM((RANK, far_slots), f32),
            pltpu.VMEM((2 * RANK, far_slots), bf16),
            pltpu.VMEM((n_cols * OWN, RANK), bf16),
            pltpu.VMEM((n_cols * OWN, RANK), bf16),
            pltpu.SemaphoreType.DMA((8,)),
            pltpu.SemaphoreType.DMA((4,)),
            pltpu.SemaphoreType.DMA((4,)),
            pltpu.SemaphoreType.DMA((n_rows - 1,)),
            pltpu.SemaphoreType.DMA((n_rows - 1,)),
            pltpu.SemaphoreType.DMA((n_cols - 1,)),
            pltpu.SemaphoreType.DMA((n_cols - 1,)),
        ],
        compiler_params=pltpu.CompilerParams(
            collective_id=0, has_side_effects=True, vmem_limit_bytes=60 * 1024 * 1024
        ),
        name="traction",
    )(
        near_count,
        far_count,
        displacement,
        positions,
        near_pairs.T,
        far_pairs.T,
        intact,
        stiffness,
        jnp.transpose(cluster_basis, (0, 2, 1)),
        jnp.transpose(far_blocks, (1, 2, 0)),
    )
    far_part = jnp.einsum("kfr,kr->kf", cluster_basis, owned, preferred_element_type=f32)
    return (base + far_part, damage)


def solution(mesh):
    both = ("rows", "cols")
    in_specs = (
        P(both, None),
        P(both, None),
        P(both, None, None),
        P(both, None),
        P(both),
        P(both, None),
        P(both),
        P(both, None, None),
        P(both, None),
        P(both, None),
    )
    out_specs = (P(both, None), P(both, None))
    return jax.shard_map(local, mesh=mesh, in_specs=in_specs, out_specs=out_specs, check_vma=False)
```

time: 70.9 us -> 47.8 us (0.67)
  the two profiles are of different devices: /device:TPU:1 before, /device:TPU:16 now
where the time goes in v3:
time: 47.8 us; the launch traced here: 47.6 us
  Pallas kernels  43 us (90%)
  between operations  1.97 us (4%)
  matrix products  1.4 us (3%)
  other arithmetic  0.66 us (1%)
  local copies, waits for them, and re-layouts  0.63 us (1%)
    pallas_call x1, Pallas kernels, local(): pl.pallas_call(functools.partial(mega, n_rows, n_cols), out_shape=(jax.Sh...  43 us
    dot_general x1, matrix products, local(): jnp.einsum('kfr,kr->kf', cluster_basis, owned, preferred_element_type=f32)  1.4 us

profile of v3, /device:TPU:16, one launch (start us, length us, event | category | flops | bytes accessed | tf_op | source)
XLA Modules:
  0.0 47.6 jit_solution(423757877302471918)
XLA Ops:
  1.9 0.0 copy-start
  1.9 43.0 %traction.1 = (f32[64,288]{1,0:T(8,128)}, f32[64,96]{1,0:T(8,128)}, bf16[64,64]{1,0:T(8,128)(2,1)}) custom-call(s32[1]{0:T(128)S(6)} %copy.18.near_count, s32[1]{0:T(128)S(6)} %copy.19.far_count, f32[64,288]{1,0:T(8,128)} %disp_hbm.1, f32[64,288]{1,0:T(8,128)} %pos_hbm.1, s32[2,256]{1,0:T(2,128)} %bitcast.12, s32[2,1024]{1,0:T(2,128)} %bitcast.11, ...), custom_call_target="tpu_custom_call" | custom-call | tf_op jit(solution)/shard_map/traction/pallas_call | solution.py:382
  44.9 0.0 copy-start.1
  44.9 0.0 copy-start.2
  45.0 0.0 copy-done
  45.0 1.4 %fusion = f32[64,1,288]{2,1,0:T(1,128)S(1)} fusion(bf16[64,288,64]{1,2,0:T(8,128)(2,1)S(1)} %copy-done, bf16[64,64,1]{1,0,2:T(8,128)(2,1)} %bitcast.10), kind=kOutput, calls=%fused_computation.1 | convolution fusion | flops 2359296 | bytes 2441216 | tf_op jit(solution)/shard_map/kfr,kr->kf/dot_general | solution.py:438
  46.4 0.0 copy-done.1
  46.4 0.7 %bitcast_add_fusion = f32[64,288]{1,0:T(8,128)} fusion(f32[64,288]{1,0:T(8,128)S(1)} %copy-done.1, f32[64,1,288]{2,1,0:T(1,128)S(1)} %fusion), kind=kLoop, calls=%fused_computation | loop fusion | flops 18432 | bytes 221184 | tf_op jit(solution)/shard_map/add | solution.py:439
  47.0 0.0 copy-done.2
  47.0 0.6 %copy.20 = f32[64,96]{1,0:T(8,128)} copy(f32[64,96]{1,0:T(8,128)S(1)} %copy-done.2) | data formatting | bytes 49152
Async XLA Ops:
  1.9 43.0 %copy-start = (bf16[64,288,64]{1,2,0:T(8,128)(2,1)S(1)}, bf16[64,288,64]{1,2,0:T(8,128)(2,1)}, u32[]{:S(2)}) copy-start(bf16[64,288,64]{1,2,0:T(8,128)(2,1)} %param.12) | copy-start | bytes 7077892
  44.9 1.4 %copy-start.1 = (f32[64,288]{1,0:T(8,128)S(1)}, f32[64,288]{1,0:T(8,128)}, u32[]{:S(2)}) copy-start(f32[64,288]{1,0:T(8,128)} %get-tuple-element.5) | copy-start | bytes 221188
  44.9 2.1 %copy-start.2 = (f32[64,96]{1,0:T(8,128)S(1)}, f32[64,96]{1,0:T(8,128)}, u32[]{:S(2)}) copy-start(f32[64,96]{1,0:T(8,128)} %get-tuple-element.11) | copy-start | bytes 73732

commit v4 on v3

--- a/solution.py
+++ b/solution.py
@@ -7,7 +7,7 @@
 from jax.experimental.pallas import tpu as pltpu
 from jax.sharding import PartitionSpec as P
 
-MESH = pl.DeviceIdType.MESH
+LOGICAL = pl.DeviceIdType.LOGICAL
 ELEMS = 96
 RANK = 64
 OWN = 64
@@ -37,9 +37,8 @@
     stiffness_hbm,
     basis_hbm,
     far_hbm,
-    base_out,
+    net_out,
     damage_out,
-    owned_out,
     ext_disp,
     ext_pos,
     near_pairs,
@@ -49,6 +48,8 @@
     wide,
     centred,
     left,
+    lefts,
+    sums,
     right_q,
     right_s,
     disp_rows,
@@ -59,7 +60,6 @@
     far_blocks,
     column,
     coupled,
-    split,
     partial,
     arrived,
     local_sem,
@@ -74,12 +74,11 @@
     i, j = lax.axis_index("rows"), lax.axis_index("cols")
     me = i * n_cols + j
     devices = n_rows * n_cols
-    after = (me + 1) % devices
-    before = (me + devices - 1) % devices
-    next_id = (after // n_cols, after % n_cols)
-    last_id = (before // n_cols, before % n_cols)
-    row_peers = [((i + d) % n_rows, j) for d in range(1, n_rows)]
-    col_peers = [(i, (j + d) % n_cols) for d in range(1, n_cols)]
+    next_id = lax.rem(me + 1, devices)
+    last_id = lax.rem(me + devices - 1, devices)
+    row_peers = [lax.rem(me + d * n_cols, devices) for d in range(1, n_rows)]
+    col_places = [lax.rem(j + d, n_cols) for d in range(1, n_cols)]
+    col_peers = [i * n_cols + place for place in col_places]
 
     own = pl.ds(0, OWN)
     loads = [
@@ -102,7 +101,7 @@
     barrier = pltpu.get_barrier_semaphore()
     peers = row_peers + col_peers + [next_id, last_id]
     for peer in peers:
-        pl.semaphore_signal(barrier, inc=1, device_id=peer, device_id_type=MESH)
+        pl.semaphore_signal(barrier, inc=1, device_id=peer, device_id_type=LOGICAL)
 
     for copy in loads[:3]:
         copy.wait()
@@ -124,6 +123,9 @@
 
     def rows_of(n, stride):
         return pl.ds(n, GROUPS, stride=stride)
+
+    def block_of(n):
+        return slice(GROUPS * n, GROUPS * (n + 1))
 
     def widen(n, ext, c, halo):
         wide[n, 2 : OWN + 2, 0:ELEMS] = ext[0:OWN, lanes_of(c)]
@@ -148,10 +150,10 @@
                 for c in range(3):
                     centred[c, rows_of(m, 4), :] = x[c]
                     for n, (a, _) in enumerate(PIECES):
-                        left[rows_of(24 * m + 3 * n + c, 96), :] = parts[c][a]
+                        left[m, block_of(3 * n + c), :] = parts[c][a]
                 for n in range(3):
-                    left[rows_of(24 * m + 18 + n, 96), :] = one
-                    left[rows_of(24 * m + 21 + n, 96), :] = norm[n]
+                    left[m, block_of(18 + n), :] = one
+                    left[m, block_of(21 + n), :] = norm[n]
 
         def packed(n, half):
             a0, a1, a2, a3 = [wide[n, rows_of(4 * half + m, 4), :][:, :ELEMS] for m in range(4)]
@@ -164,6 +166,8 @@
         for half in range(2):
             sources = [packed(n, half) for n in range(6)]
             for v in range(3):
+                if halo and v == 2 - 2 * half:
+                    continue
                 w = 3 * half + v
                 y = [sources[c][v] - centre[c] for c in range(3)]
                 u = [sources[3 + c][v] for c in range(3)]
@@ -173,18 +177,18 @@
                 inner = thirds(y[0] * u[0] + y[1] * u[1] + y[2] * u[2])
                 for c in range(3):
                     for n, (_, b) in enumerate(PIECES):
-                        right_q[w, rows_of(3 * n + c, 24), :] = -2.0 * y_parts[c][b]
-                        right_s[w, rows_of(3 * n + c, 24), :] = u_parts[c][b]
-                    disp_rows[w, rows_of(c, 8), :] = u[c]
-                    pos_rows[w, rows_of(c, 8), :] = 3.0 * y[c]
+                        right_q[w, block_of(3 * n + c), :] = -2.0 * y_parts[c][b]
+                        right_s[w, block_of(3 * n + c), :] = u_parts[c][b]
+                    disp_rows[w, block_of(c), :] = u[c]
+                    pos_rows[w, block_of(c), :] = 3.0 * y[c]
                 for n in range(3):
-                    right_q[w, rows_of(18 + n, 24), :] = norm[n]
-                    right_s[w, rows_of(18 + n, 24), :] = -inner[n]
-                    right_q[w, rows_of(21 + n, 24), :] = one
-                    right_s[w, rows_of(21 + n, 24), :] = none
+                    right_q[w, block_of(18 + n), :] = norm[n]
+                    right_s[w, block_of(18 + n), :] = -inner[n]
+                    right_q[w, block_of(21 + n), :] = one
+                    right_s[w, block_of(21 + n), :] = none
                 for n in range(3, 8):
-                    disp_rows[w, rows_of(n, 8), :] = none
-                    pos_rows[w, rows_of(n, 8), :] = 3.0 * one if n == 3 else none
+                    disp_rows[w, block_of(n), :] = none
+                    pos_rows[w, block_of(n), :] = 3.0 * one if n == 3 else none
 
     wide[...] = jnp.zeros_like(wide)
     build(False)
@@ -211,39 +215,47 @@
     def three_rows(x):
         return jnp.concatenate(thirds(x) + (jnp.zeros_like(x),), axis=0).astype(bf16)
 
+    def turn(g, _):
+        group = pl.ds(g, 24, stride=GROUPS)
+        for m in range(4):
+            lefts[4 * g + m] = left[m, group, :].T[:ELEMS].astype(bf16)
+        return 0
+
+    lax.fori_loop(0, GROUPS, turn, 0)
+
     def near_groups(first, last):
         def near_group(g, _):
-            top = pl.multiple_of(g * 24, 8)
-            right = [
-                jnp.concatenate([right_q[w, pl.ds(top, 24), :], right_s[w, pl.ds(top, 24), :]], axis=1).astype(bf16)
-                for w in range(6)
-            ]
-            eight = pl.ds(pl.multiple_of(g * 8, 8), 8)
+            group = pl.ds(g, 24, stride=GROUPS)
+            eight = pl.ds(g, 8, stride=GROUPS)
+            rights, rows = [], []
+            for w in range(6):
+                rights.append(jnp.concatenate([right_q[w, group, :], right_s[w, group, :]], axis=1).astype(bf16))
+                u_rows = three_rows(disp_rows[w, eight, :])
+                y_rows = three_rows(pos_rows[w, eight, :])
+                rows.append(jnp.concatenate([u_rows, u_rows, y_rows, y_rows], axis=1))
+            totals = [None] * 4
+            for n in range(5):
+                for pair in range(2):
+                    w = n + pair
+                    seen = [m for m in (2 * pair, 2 * pair + 1) if w in SEEN[m]]
+                    mine = jnp.concatenate([lefts[4 * g + m] for m in seen], axis=0)
+                    both = jnp.dot(mine, rights[w], preferred_element_type=f32)
+                    values = []
+                    for at, m in enumerate(seen):
+                        part = both[at * ELEMS : (at + 1) * ELEMS]
+                        inverse = lax.rsqrt(jnp.maximum(part[:, :LANES], core_square))
+                        square = inverse * inverse
+                        cube = square * (inverse * weights[w, pl.ds(4 * g + m, 1), :])
+                        pull = (part[:, LANES:] * square) * cube
+                        values.append(jnp.concatenate(halves(cube) + halves(pull), axis=1))
+                    added = lax.dot_general(
+                        jnp.concatenate(values, axis=0), rows[w], (((1,), (1,)), ((), ())), preferred_element_type=f32
+                    )
+                    for at, m in enumerate(seen):
+                        piece = added[at * ELEMS : (at + 1) * ELEMS]
+                        totals[m] = piece if totals[m] is None else totals[m] + piece
             for m in range(4):
-                mine = left[pl.ds(pl.multiple_of(g * 96 + 24 * m, 8), 24), :]
-                mine = mine.T[:ELEMS].astype(bf16)
-                total = jnp.zeros((ELEMS, 32), f32)
-                for w in SEEN[m]:
-                    both = jnp.dot(mine, right[w], preferred_element_type=f32)
-                    inverse = lax.rsqrt(jnp.maximum(both[:, :LANES], core_square))
-                    square = inverse * inverse
-                    cube = square * inverse
-                    pull = both[:, LANES:] * square * cube
-                    values = jnp.concatenate(halves(cube) + halves(pull), axis=1)
-                    count = jnp.broadcast_to(weights[w, pl.ds(4 * g + m, 1), :], (8, LANES))
-                    u_rows = three_rows(disp_rows[w, eight, :] * count)
-                    y_rows = three_rows(pos_rows[w, eight, :] * count)
-                    total = total + lax.dot_general(
-                        values,
-                        jnp.concatenate([u_rows, u_rows, y_rows, y_rows], axis=1),
-                        (((1,), (1,)), ((), ())),
-                        preferred_element_type=f32,
-                    )
-                total = total.T
-                total = total[0:8] + total[8:16] + total[16:24]
-                for c in range(3):
-                    row = pl.ds(4 * g + m, 1)
-                    near_rows[c, row, 0:ELEMS] = total[c : c + 1] - centred[c, row, 0:ELEMS] * total[3:4]
+                sums[4 * g + m] = totals[m]
             return 0
 
         lax.fori_loop(first, last, near_group, 0)
@@ -252,10 +264,13 @@
 
     def project(block, coeff):
         top = pl.multiple_of(block * 8, 8)
-        rows = ext_disp[pl.ds(top, 8), :].astype(bf16).astype(f32)
+        rows = ext_disp[pl.ds(top, 8), :].astype(bf16)
         lane = lax.broadcasted_iota(jnp.int32, (RANK, OWN), 1)
         for n in range(8):
-            product = basis[top + n].astype(f32) * rows[n : n + 1, :]
+            product = basis[top + n] * rows[n : n + 1, :]
+            product = product[:, :LANES].astype(f32) + product[:, LANES : 2 * LANES].astype(f32) + jnp.concatenate(
+                [product[:, 2 * LANES :].astype(f32), jnp.zeros((RANK, 3 * LANES - WIDTH), f32)], axis=1
+            )
             coeff = jnp.where(lane == top + n, jnp.sum(product, axis=1, keepdims=True), coeff)
         return coeff
 
@@ -268,7 +283,7 @@
 
     def remote(src, dst, send, recv, peer):
         return pltpu.make_async_remote_copy(
-            src_ref=src, dst_ref=dst, send_sem=send, recv_sem=recv, device_id=peer, device_id_type=MESH
+            src_ref=src, dst_ref=dst, send_sem=send, recv_sem=recv, device_id=peer, device_id_type=LOGICAL
         )
 
     mine = column.at[own_rows, :]
@@ -292,35 +307,38 @@
     far_slots = far_pairs.shape[1]
     sources = n_rows * OWN
 
+    wide_block = 2 * LANES
+    fold = lax.broadcasted_iota(jnp.int32, (16, 256), 0) == lax.broadcasted_iota(jnp.int32, (16, 256), 1) // 16
+    fold = fold.astype(f32).astype(bf16)
+
     def couple(block, _):
-        first = pl.multiple_of(block * LANES, LANES)
-        source = far_pairs[1:2, pl.ds(first, LANES)]
-        alive = lax.broadcasted_iota(jnp.int32, (1, LANES), 1) + first < far_count[0]
+        first = pl.multiple_of(block * wide_block, wide_block)
+        source = far_pairs[1:2, pl.ds(first, wide_block)]
+        alive = lax.broadcasted_iota(jnp.int32, (1, wide_block), 1) + first < far_count[0]
         source = jnp.where(alive, source, -1)
-        chosen = (lax.broadcasted_iota(jnp.int32, (sources, LANES), 0) == source).astype(f32).astype(bf16)
-        gathered = jnp.dot(column_turned, chosen, preferred_element_type=f32)
+        chosen = (lax.broadcasted_iota(jnp.int32, (sources, wide_block), 0) == source).astype(f32).astype(bf16)
+        gathered = jnp.dot(column_turned, chosen, preferred_element_type=f32).astype(bf16)
 
         def ranks(part, _):
-            top = pl.multiple_of(part * 8, 8)
-            blocks = far_blocks[pl.ds(top, 8), :, pl.ds(first, LANES)].astype(f32)
-            coupled[pl.ds(top, 8), pl.ds(first, LANES)] = jnp.sum(blocks * gathered[None], axis=1)
+            top = pl.multiple_of(part * 16, 16)
+            summed = []
+            for n in range(16):
+                product = far_blocks[top + n, :, pl.ds(first, wide_block)] * gathered
+                summed.append((product[0:16] + product[16:32]) + (product[32:48] + product[48:64]))
+            whole = jnp.dot(fold, jnp.concatenate(summed, axis=0), preferred_element_type=f32)
+            coupled[pl.ds(top, 16), pl.ds(first, wide_block)] = whole.astype(bf16)
             return 0
 
-        return lax.fori_loop(0, RANK // 8, ranks, 0)
-
-    lax.fori_loop(0, far_slots // LANES, couple, 0)
-    whole = coupled[...]
-    high = whole.astype(bf16)
-    split[0:RANK, :] = high
-    split[RANK : 2 * RANK, :] = (whole - high.astype(f32)).astype(bf16)
+        return lax.fori_loop(0, RANK // 16, ranks, 0)
+
+    lax.fori_loop(0, far_slots // wide_block, couple, 0)
 
     def collect(block, _):
         first = pl.multiple_of(block * LANES, LANES)
         chosen = (lax.broadcasted_iota(jnp.int32, (LANES, far_slots), 0) + first == far_pairs[0:1, :]).astype(f32)
-        both = lax.dot_general(
-            chosen.astype(bf16), split[...], (((1,), (1,)), ((), ())), preferred_element_type=f32
-        )
-        partial[pl.ds(first, LANES), :] = (both[:, :RANK] + both[:, RANK:]).astype(bf16)
+        partial[pl.ds(first, LANES), :] = lax.dot_general(
+            chosen.astype(bf16), coupled[...], (((1,), (1,)), ((), ())), preferred_element_type=f32
+        ).astype(bf16)
         return 0
 
     lax.fori_loop(0, n_cols * OWN // LANES, collect, 0)
@@ -331,7 +349,7 @@
     here = pl.ds(pl.multiple_of(j * OWN, OWN), OWN)
     scatters = []
     for d, peer in enumerate(col_peers):
-        block = partial.at[pl.ds(pl.multiple_of(peer[1] * OWN, OWN), OWN), :]
+        block = partial.at[pl.ds(pl.multiple_of(col_places[d] * OWN, OWN), OWN), :]
         scatters.append(remote(block, arrived.at[here, :], scatter_send.at[d], scatter_recv.at[d], peer))
     for copy in scatters:
         copy.start()
@@ -343,6 +361,16 @@
     near_groups(*THIRD)
     near_groups(0, 1)
 
+    def settle(block, _):
+        for n in range(4):
+            row = pl.ds(4 * block + n, 1)
+            total = sums[4 * block + n].T
+            total = total[0:8] + total[8:16] + total[16:24]
+            for c in range(3):
+                near_rows[c, row, 0:ELEMS] = total[c : c + 1] - centred[c, row, 0:ELEMS] * total[3:4]
+        return 0
+
+    lax.fori_loop(0, OWN // 4, settle, 0)
     parts = [near_rows[c, :, 0:ELEMS] for c in range(3)]
     u = [ext_disp[0:OWN, lanes_of(c)] for c in range(3)]
     separation = jnp.sqrt(1.0 + (u[0] * u[0] + u[1] * u[1] + u[2] * u[2]))
@@ -351,14 +379,22 @@
     damage = whole_element * softened + (1.0 - whole_element)
     damage_out[...] = damage
     held = (1.0 - damage) * stiffness[...]
-    base_out[...] = jnp.concatenate([parts[c] - held * u[c] for c in range(3)], axis=1)
+    base = jnp.concatenate([parts[c] - held * u[c] for c in range(3)], axis=1)
 
     for copy in scatters:
         copy.wait()
     owned = arrived[0:OWN, :].astype(f32)
     for n in range(1, n_cols):
         owned = owned + arrived[n * OWN : (n + 1) * OWN, :].astype(f32)
-    owned_out[...] = owned.astype(bf16)
+    owned = owned.T
+    for block in range(OWN // 16):
+        summed = []
+        for n in range(16):
+            k = 16 * block + n
+            product = basis[k] * owned[:, k : k + 1].astype(bf16)
+            summed.append((product[0:16] + product[16:32]) + (product[32:48] + product[48:64]))
+        far = jnp.dot(fold, jnp.concatenate(summed, axis=0), preferred_element_type=f32)
+        net_out[16 * block : 16 * block + 16, :] = base[16 * block : 16 * block + 16] + far
 
 
 def local(
@@ -379,15 +415,14 @@
     vmem = pl.BlockSpec(memory_space=pltpu.VMEM)
     smem = pl.BlockSpec(memory_space=pltpu.SMEM)
     hbm = pl.BlockSpec(memory_space=pltpu.HBM)
-    base, damage, owned = pl.pallas_call(
+    return pl.pallas_call(
         functools.partial(mega, n_rows, n_cols),
         out_shape=(
             jax.ShapeDtypeStruct((OWN, WIDTH), f32),
             jax.ShapeDtypeStruct((OWN, ELEMS), f32),
-            jax.ShapeDtypeStruct((OWN, RANK), bf16),
         ),
         in_specs=[smem, smem] + [hbm] * 8,
-        out_specs=(vmem, vmem, vmem),
+        out_specs=(vmem, vmem),
         scratch_shapes=[
             pltpu.VMEM((2 * OWN, WIDTH), f32),
             pltpu.VMEM((2 * OWN, WIDTH), f32),
@@ -397,7 +432,9 @@
             pltpu.VMEM((OWN, ELEMS), f32),
             pltpu.VMEM((6, OWN + 8, LANES), f32),
             pltpu.VMEM((3, OWN, LANES), f32),
-            pltpu.VMEM((24 * OWN, LANES), f32),
+            pltpu.VMEM((4, 24 * GROUPS, LANES), f32),
+            pltpu.VMEM((OWN, ELEMS, 24), bf16),
+            pltpu.VMEM((OWN, ELEMS, 32), f32),
             pltpu.VMEM((6, 24 * GROUPS, LANES), f32),
             pltpu.VMEM((6, 24 * GROUPS, LANES), f32),
             pltpu.VMEM((6, 8 * GROUPS, LANES), f32),
@@ -407,8 +444,7 @@
             pltpu.VMEM((OWN, RANK, WIDTH), bf16),
             pltpu.VMEM((RANK, RANK, far_slots), bf16),
             pltpu.VMEM((n_rows * OWN, RANK), bf16),
-            pltpu.VMEM((RANK, far_slots), f32),
-            pltpu.VMEM((2 * RANK, far_slots), bf16),
+            pltpu.VMEM((RANK, far_slots), bf16),
             pltpu.VMEM((n_cols * OWN, RANK), bf16),
             pltpu.VMEM((n_cols * OWN, RANK), bf16),
             pltpu.SemaphoreType.DMA((8,)),
@@ -435,8 +471,6 @@
         jnp.transpose(cluster_basis, (0, 2, 1)),
         jnp.transpose(far_blocks, (1, 2, 0)),
     )
-    far_part = jnp.einsum("kfr,kr->kf", cluster_basis, owned, preferred_element_type=f32)
-    return (base + far_part, damage)
 
 
 def solution(mesh):

time: 47.8 us -> 47.3 us (0.990)
  local copies, waits for them, and re-layouts: 0.63 us -> 2.91 us
  matrix products: 1.4 us -> 0 us
  Pallas kernels: 43 us -> 42.3 us
  other arithmetic: 0.66 us -> 0 us
    unnamed x7 -> x2, local copies, waits for them, and re-layouts: 0.63 us -> 2.91 us
    dot_general x1 -> x0, matrix products: 1.4 us -> none  [local(): jnp.einsum('kfr,kr->kf', cluster_basis, owned, preferred_element_type=f32)]
    pallas_call x1, Pallas kernels: 43 us -> 42.3 us  [local(): pl.pallas_call(functools.partial(mega, n_rows, n_cols), out_shape=(jax.Sh...]
    add x1 -> x0, other arithmetic: 0.66 us -> none  [local(): return (base + far_part, damage)]
where the time goes in v4:
time: 47.3 us; the launch traced here: 47.1 us
  Pallas kernels  42.3 us (89%)
  local copies, waits for them, and re-layouts  2.91 us (6%)
  between operations  1.93 us (4%)
    pallas_call x1, Pallas kernels, local(): pl.pallas_call(functools.partial(mega, n_rows, n_cols), out_shape=(jax.Sh...  42.3 us
    unnamed x2, local copies, waits for them, and re-layouts  2.91 us

profile of v4, /device:TPU:16, one launch (start us, length us, event | category | flops | bytes accessed | tf_op | source)
XLA Modules:
  0.0 47.1 jit_solution(15147893065828713716)
XLA Ops:
  1.9 42.3 %traction.1 = (f32[64,288]{1,0:T(8,128)}, f32[64,96]{1,0:T(8,128)}) custom-call(s32[1]{0:T(128)S(6)} %copy.14.near_count, s32[1]{0:T(128)S(6)} %copy.15.far_count, f32[64,288]{1,0:T(8,128)} %disp_hbm.1, f32[64,288]{1,0:T(8,128)} %pos_hbm.1, s32[2,256]{1,0:T(2,128)} %bitcast.7, s32[2,1024]{1,0:T(2,128)} %bitcast.6, s32[64,96]{1,0:T(8,128)} %intact_hbm.1, ...), custom_call_target="tpu_custom_call" | custom-call | tf_op jit(solution)/shard_map/traction/pallas_call | solution.py:418
  44.2 1.5 %copy.16 = f32[64,288]{1,0:T(8,128)} copy(f32[64,288]{1,0:T(8,128)} %get-tuple-element.4) | data formatting | bytes 147456
  45.7 1.4 %copy.17 = f32[64,96]{1,0:T(8,128)} copy(f32[64,96]{1,0:T(8,128)} %get-tuple-element.5) | data formatting | bytes 49152

commit v5 on v4

--- a/solution.py
+++ b/solution.py
@@ -19,8 +19,8 @@
 
 PIECES = ((0, 0), (0, 1), (1, 0), (1, 1), (0, 2), (2, 0))
 SEEN = (range(0, 4), range(0, 5), range(1, 6), range(2, 6))
-FIRST = (1, 6)
-SECOND = (6, 11)
+FIRST = (1, 7)
+SECOND = (7, 11)
 THIRD = (11, 16)
 
 
@@ -179,14 +179,16 @@
                     for n, (_, b) in enumerate(PIECES):
                         right_q[w, block_of(3 * n + c), :] = -2.0 * y_parts[c][b]
                         right_s[w, block_of(3 * n + c), :] = u_parts[c][b]
-                    disp_rows[w, block_of(c), :] = u[c]
-                    pos_rows[w, block_of(c), :] = 3.0 * y[c]
+                    triple = thirds(3.0 * y[c])
+                    for n in range(2):
+                        disp_rows[w, block_of(4 * n + c), :] = u_parts[c][n]
+                        pos_rows[w, block_of(4 * n + c), :] = triple[n]
                 for n in range(3):
                     right_q[w, block_of(18 + n), :] = norm[n]
                     right_s[w, block_of(18 + n), :] = -inner[n]
                     right_q[w, block_of(21 + n), :] = one
                     right_s[w, block_of(21 + n), :] = none
-                for n in range(3, 8):
+                for n in (3, 7):
                     disp_rows[w, block_of(n), :] = none
                     pos_rows[w, block_of(n), :] = 3.0 * one if n == 3 else none
 
@@ -212,37 +214,43 @@
         high = x.astype(bf16)
         return high, (x - high.astype(f32)).astype(bf16)
 
-    def three_rows(x):
-        return jnp.concatenate(thirds(x) + (jnp.zeros_like(x),), axis=0).astype(bf16)
-
-    def turn(g, _):
-        group = pl.ds(g, 24, stride=GROUPS)
+    def turn(g):
         for m in range(4):
-            lefts[4 * g + m] = left[m, group, :].T[:ELEMS].astype(bf16)
-        return 0
-
-    lax.fori_loop(0, GROUPS, turn, 0)
+            lefts[4 * g + m] = left[m, pl.ds(g, 24, stride=GROUPS), :].T[:ELEMS].astype(bf16)
+
+    def settle(g):
+        for m in range(4):
+            row = pl.ds(4 * g + m, 1)
+            total = sums[4 * g + m].T
+            total = total[0:4] + total[4:8]
+            for c in range(3):
+                near_rows[c, row, 0:ELEMS] = total[c : c + 1] - centred[c, row, 0:ELEMS] * total[3:4]
+
+    turn(0)
+    turn(1)
 
     def near_groups(first, last):
         def near_group(g, _):
             group = pl.ds(g, 24, stride=GROUPS)
             eight = pl.ds(g, 8, stride=GROUPS)
-            rights, rows = [], []
+            rows, boths = [], []
             for w in range(6):
-                rights.append(jnp.concatenate([right_q[w, group, :], right_s[w, group, :]], axis=1).astype(bf16))
-                u_rows = three_rows(disp_rows[w, eight, :])
-                y_rows = three_rows(pos_rows[w, eight, :])
+                right = jnp.concatenate([right_q[w, group, :], right_s[w, group, :]], axis=1).astype(bf16)
+                u_rows = disp_rows[w, eight, :].astype(bf16)
+                y_rows = pos_rows[w, eight, :].astype(bf16)
                 rows.append(jnp.concatenate([u_rows, u_rows, y_rows, y_rows], axis=1))
+                seen = [m for m in range(4) if w in SEEN[m]]
+                mine = jnp.concatenate([lefts[4 * g + m] for m in seen], axis=0)
+                both = jnp.dot(mine, right, preferred_element_type=f32)
+                boths.append({m: both[at * ELEMS : (at + 1) * ELEMS] for at, m in enumerate(seen)})
             totals = [None] * 4
             for n in range(5):
                 for pair in range(2):
                     w = n + pair
                     seen = [m for m in (2 * pair, 2 * pair + 1) if w in SEEN[m]]
-                    mine = jnp.concatenate([lefts[4 * g + m] for m in seen], axis=0)
-                    both = jnp.dot(mine, rights[w], preferred_element_type=f32)
                     values = []
-                    for at, m in enumerate(seen):
-                        part = both[at * ELEMS : (at + 1) * ELEMS]
+                    for m in seen:
+                        part = boths[w][m]
                         inverse = lax.rsqrt(jnp.maximum(part[:, :LANES], core_square))
                         square = inverse * inverse
                         cube = square * (inverse * weights[w, pl.ds(4 * g + m, 1), :])
@@ -254,11 +262,14 @@
                     for at, m in enumerate(seen):
                         piece = added[at * ELEMS : (at + 1) * ELEMS]
                         totals[m] = piece if totals[m] is None else totals[m] + piece
+            settle(jnp.maximum(g - 1, 0))
             for m in range(4):
                 sums[4 * g + m] = totals[m]
+            turn(jnp.minimum(g + 1, GROUPS - 1))
             return 0
 
         lax.fori_loop(first, last, near_group, 0)
+        settle(last - 1)
 
     loads[3].wait()
 
@@ -275,8 +286,13 @@
         return coeff
 
     coeff = lax.fori_loop(0, OWN // 8, project, jnp.zeros((RANK, OWN), f32))
-    own_rows = pl.ds(pl.multiple_of(i * OWN, OWN), OWN)
-    column[own_rows, :] = coeff.astype(bf16)
+    half = OWN // 2
+
+    def pack(block):
+        return jnp.concatenate([block[:half], block[half:]], axis=1).astype(bf16)
+
+    own_rows = pl.ds(pl.multiple_of(i * half, half), half)
+    column[own_rows, :] = pack(coeff)
 
     near_groups(*FIRST)
     pl.semaphore_wait(barrier, len(peers))
@@ -303,13 +319,32 @@
         copy.wait()
     for copy in loads[4:]:
         copy.wait()
-    column_turned = jnp.concatenate([column[n * OWN : (n + 1) * OWN, :] for n in range(n_rows)], axis=1)
+    tops = [column[n * half : (n + 1) * half, :RANK] for n in range(n_rows)]
+    bottoms = [column[n * half : (n + 1) * half, RANK:] for n in range(n_rows)]
+    column_turned = jnp.concatenate(
+        [jnp.concatenate(tops, axis=1), jnp.concatenate(bottoms, axis=1)], axis=0
+    )
     far_slots = far_pairs.shape[1]
     sources = n_rows * OWN
 
     wide_block = 2 * LANES
-    fold = lax.broadcasted_iota(jnp.int32, (16, 256), 0) == lax.broadcasted_iota(jnp.int32, (16, 256), 1) // 16
-    fold = fold.astype(f32).astype(bf16)
+    sublane = lax.broadcasted_iota(jnp.int32, (8, wide_block), 0)
+
+    def merge(blocks):
+        reach = 4
+        while len(blocks) > 1:
+            upper = sublane // reach % 2 == 0
+            count = len(blocks) // 2
+            pairs = [(blocks[n], blocks[n + count]) for n in range(count)]
+            blocks = []
+            for x, y in pairs:
+                crossed = jnp.where(upper, y, x)
+                moved = pltpu.roll(crossed, reach, axis=0)
+                if reach < 4:
+                    moved = jnp.where(upper, pltpu.roll(crossed, 8 - reach, axis=0), moved)
+                blocks.append(jnp.where(upper, x, y) + moved)
+            reach //= 2
+        return blocks[0]
 
     def couple(block, _):
         first = pl.multiple_of(block * wide_block, wide_block)
@@ -324,8 +359,9 @@
             summed = []
             for n in range(16):
                 product = far_blocks[top + n, :, pl.ds(first, wide_block)] * gathered
-                summed.append((product[0:16] + product[16:32]) + (product[32:48] + product[48:64]))
-            whole = jnp.dot(fold, jnp.concatenate(summed, axis=0), preferred_element_type=f32)
+                product = ((product[0:16] + product[16:32]) + (product[32:48] + product[48:64])).astype(f32)
+                summed.append(product[0:8] + product[8:16])
+            whole = jnp.concatenate([merge(summed[:8]), merge(summed[8:])], axis=0)
             coupled[pl.ds(top, 16), pl.ds(first, wide_block)] = whole.astype(bf16)
             return 0
 
@@ -334,22 +370,25 @@
     lax.fori_loop(0, far_slots // wide_block, couple, 0)
 
     def collect(block, _):
-        first = pl.multiple_of(block * LANES, LANES)
-        chosen = (lax.broadcasted_iota(jnp.int32, (LANES, far_slots), 0) + first == far_pairs[0:1, :]).astype(f32)
-        partial[pl.ds(first, LANES), :] = lax.dot_general(
-            chosen.astype(bf16), coupled[...], (((1,), (1,)), ((), ())), preferred_element_type=f32
-        ).astype(bf16)
+        first = pl.multiple_of(block * wide_block, wide_block)
+        chosen = lax.broadcasted_iota(jnp.int32, (wide_block, far_slots), 0) + first == far_pairs[0:1, :]
+        found = lax.dot_general(
+            chosen.astype(f32).astype(bf16), coupled[...], (((1,), (1,)), ((), ())), preferred_element_type=f32
+        )
+        for n in range(wide_block // OWN):
+            to = pl.multiple_of(block * (wide_block // 2) + n * half, half)
+            partial[pl.ds(to, half), :] = pack(found[n * OWN : (n + 1) * OWN])
         return 0
 
-    lax.fori_loop(0, n_cols * OWN // LANES, collect, 0)
+    lax.fori_loop(0, n_cols * OWN // wide_block, collect, 0)
 
     for copy in halos:
         copy.wait()
 
-    here = pl.ds(pl.multiple_of(j * OWN, OWN), OWN)
+    here = pl.ds(pl.multiple_of(j * half, half), half)
     scatters = []
     for d, peer in enumerate(col_peers):
-        block = partial.at[pl.ds(pl.multiple_of(col_places[d] * OWN, OWN), OWN), :]
+        block = partial.at[pl.ds(pl.multiple_of(col_places[d] * half, half), half), :]
         scatters.append(remote(block, arrived.at[here, :], scatter_send.at[d], scatter_recv.at[d], peer))
     for copy in scatters:
         copy.start()
@@ -361,16 +400,6 @@
     near_groups(*THIRD)
     near_groups(0, 1)
 
-    def settle(block, _):
-        for n in range(4):
-            row = pl.ds(4 * block + n, 1)
-            total = sums[4 * block + n].T
-            total = total[0:8] + total[8:16] + total[16:24]
-            for c in range(3):
-                near_rows[c, row, 0:ELEMS] = total[c : c + 1] - centred[c, row, 0:ELEMS] * total[3:4]
-        return 0
-
-    lax.fori_loop(0, OWN // 4, settle, 0)
     parts = [near_rows[c, :, 0:ELEMS] for c in range(3)]
     u = [ext_disp[0:OWN, lanes_of(c)] for c in range(3)]
     separation = jnp.sqrt(1.0 + (u[0] * u[0] + u[1] * u[1] + u[2] * u[2]))
@@ -383,10 +412,13 @@
 
     for copy in scatters:
         copy.wait()
-    owned = arrived[0:OWN, :].astype(f32)
+    owned = arrived[0:half, :].astype(f32)
     for n in range(1, n_cols):
-        owned = owned + arrived[n * OWN : (n + 1) * OWN, :].astype(f32)
+        owned = owned + arrived[n * half : (n + 1) * half, :].astype(f32)
     owned = owned.T
+    owned = jnp.concatenate([owned[:RANK], owned[RANK:]], axis=1)
+    fold = lax.broadcasted_iota(jnp.int32, (16, 256), 0) == lax.broadcasted_iota(jnp.int32, (16, 256), 1) // 16
+    fold = fold.astype(f32).astype(bf16)
     for block in range(OWN // 16):
         summed = []
         for n in range(16):
@@ -434,7 +466,7 @@
             pltpu.VMEM((3, OWN, LANES), f32),
             pltpu.VMEM((4, 24 * GROUPS, LANES), f32),
             pltpu.VMEM((OWN, ELEMS, 24), bf16),
-            pltpu.VMEM((OWN, ELEMS, 32), f32),
+            pltpu.VMEM((OWN, ELEMS, 8), f32),
             pltpu.VMEM((6, 24 * GROUPS, LANES), f32),
             pltpu.VMEM((6, 24 * GROUPS, LANES), f32),
             pltpu.VMEM((6, 8 * GROUPS, LANES), f32),
@@ -443,10 +475,10 @@
             pltpu.VMEM((3, OWN, LANES), f32),
             pltpu.VMEM((OWN, RANK, WIDTH), bf16),
             pltpu.VMEM((RANK, RANK, far_slots), bf16),
-            pltpu.VMEM((n_rows * OWN, RANK), bf16),
+            pltpu.VMEM((n_rows * OWN // 2, 2 * RANK), bf16),
             pltpu.VMEM((RANK, far_slots), bf16),
-            pltpu.VMEM((n_cols * OWN, RANK), bf16),
-            pltpu.VMEM((n_cols * OWN, RANK), bf16),
+            pltpu.VMEM((n_cols * OWN // 2, 2 * RANK), bf16),
+            pltpu.VMEM((n_cols * OWN // 2, 2 * RANK), bf16),
             pltpu.SemaphoreType.DMA((8,)),
             pltpu.SemaphoreType.DMA((4,)),
             pltpu.SemaphoreType.DMA((4,)),

time: 47.3 us -> 38.5 us (0.81)
  the two profiles are of different devices: /device:TPU:16 before, /device:TPU:1 now
where the time goes in v5:
time: 38.5 us; the launch traced here: 38.3 us
  Pallas kernels  33.5 us (87%)
  local copies, waits for them, and re-layouts  2.91 us (8%)
  between operations  1.93 us (5%)
    pallas_call x1, Pallas kernels, local(): pl.pallas_call(functools.partial(mega, n_rows, n_cols), out_shape=(jax.Sh...  33.5 us
    unnamed x2, local copies, waits for them, and re-layouts  2.91 us

profile of v5, /device:TPU:1, one launch (start us, length us, event | category | flops | bytes accessed | tf_op | source)
XLA Modules:
  0.0 38.3 jit_solution(12543296674730716523)
XLA Ops:
  1.9 33.5 %traction.1 = (f32[64,288]{1,0:T(8,128)}, f32[64,96]{1,0:T(8,128)}) custom-call(s32[1]{0:T(128)S(6)} %copy.14.near_count, s32[1]{0:T(128)S(6)} %copy.15.far_count, f32[64,288]{1,0:T(8,128)} %disp_hbm.1, f32[64,288]{1,0:T(8,128)} %pos_hbm.1, s32[2,256]{1,0:T(2,128)} %bitcast.7, s32[2,1024]{1,0:T(2,128)} %bitcast.6, s32[64,96]{1,0:T(8,128)} %intact_hbm.1, ...), custom_call_target="tpu_custom_call" | custom-call | tf_op jit(solution)/shard_map/traction/pallas_call | solution.py:450
  35.4 1.5 %copy.16 = f32[64,288]{1,0:T(8,128)} copy(f32[64,288]{1,0:T(8,128)} %get-tuple-element.4) | data formatting | bytes 147456
  36.9 1.4 %copy.17 = f32[64,96]{1,0:T(8,128)} copy(f32[64,96]{1,0:T(8,128)} %get-tuple-element.5) | data formatting | bytes 49152

commit v6 on v5

--- a/solution.py
+++ b/solution.py
@@ -19,9 +19,6 @@
 
 PIECES = ((0, 0), (0, 1), (1, 0), (1, 1), (0, 2), (2, 0))
 SEEN = (range(0, 4), range(0, 5), range(1, 6), range(2, 6))
-FIRST = (1, 7)
-SECOND = (7, 11)
-THIRD = (11, 16)
 
 
 def mega(
@@ -294,7 +291,10 @@
     own_rows = pl.ds(pl.multiple_of(i * half, half), half)
     column[own_rows, :] = pack(coeff)
 
-    near_groups(*FIRST)
+    z = lax.rem(j, 4) * 2 + i // (n_rows // 2)
+    sent = 8 - jnp.minimum(z, 4) * 3 // 2
+    gathered_at = sent + jnp.where(z == 0, 4, 5)
+    near_groups(1, sent)
     pl.semaphore_wait(barrier, len(peers))
 
     def remote(src, dst, send, recv, peer):
@@ -313,7 +313,7 @@
     for copy in gathers + halos:
         copy.start()
 
-    near_groups(*SECOND)
+    near_groups(sent, gathered_at)
 
     for copy in gathers:
         copy.wait()
@@ -397,7 +397,7 @@
     ext_disp[OWN : OWN + 8, :] = jnp.where(me == devices - 1, 0.0, ext_disp[OWN : OWN + 8, :])
     ext_disp[120:128, :] = jnp.where(me == 0, 0.0, ext_disp[120:128, :])
     build(True)
-    near_groups(*THIRD)
+    near_groups(gathered_at, GROUPS)
     near_groups(0, 1)
 
     parts = [near_rows[c, :, 0:ELEMS] for c in range(3)]
@@ -453,7 +453,7 @@
             jax.ShapeDtypeStruct((OWN, WIDTH), f32),
             jax.ShapeDtypeStruct((OWN, ELEMS), f32),
         ),
-        in_specs=[smem, smem] + [hbm] * 8,
+        in_specs=[smem] * 2 + [hbm] * 8,
         out_specs=(vmem, vmem),
         scratch_shapes=[
             pltpu.VMEM((2 * OWN, WIDTH), f32),
@@ -488,20 +488,25 @@
             pltpu.SemaphoreType.DMA((n_cols - 1,)),
         ],
         compiler_params=pltpu.CompilerParams(
-            collective_id=0, has_side_effects=True, vmem_limit_bytes=60 * 1024 * 1024
+            collective_id=0, has_side_effects=True, vmem_limit_bytes=34 * 1024 * 1024
         ),
         name="traction",
     )(
         near_count,
         far_count,
-        displacement,
-        positions,
-        near_pairs.T,
-        far_pairs.T,
-        intact,
-        stiffness,
-        jnp.transpose(cluster_basis, (0, 2, 1)),
-        jnp.transpose(far_blocks, (1, 2, 0)),
+        *[
+            pltpu.with_memory_space_constraint(x, pltpu.HBM)
+            for x in (
+                displacement,
+                positions,
+                near_pairs.T,
+                far_pairs.T,
+                intact,
+                stiffness,
+                jnp.transpose(cluster_basis, (0, 2, 1)),
+                jnp.transpose(far_blocks, (1, 2, 0)),
+            )
+        ],
     )
 
 

time: 38.5 us -> 31.2 us (0.81)
  Pallas kernels: 33.5 us -> 28 us
  local copies, waits for them, and re-layouts: 2.91 us -> 1.26 us
    pallas_call x1, Pallas kernels: 33.5 us -> 28 us  [local(): pl.pallas_call(functools.partial(mega, n_rows, n_cols), out_shape=(jax.Sh...]
    unnamed x2, local copies, waits for them, and re-layouts: 2.91 us -> 1.26 us
where the time goes in v6:
time: 31.2 us; the launch traced here: 31.1 us
  Pallas kernels  28 us (90%)
  between operations  1.93 us (6%)
  local copies, waits for them, and re-layouts  1.26 us (4%)
    pallas_call x1, Pallas kernels, local(): pl.pallas_call(functools.partial(mega, n_rows, n_cols), out_shape=(jax.Sh...  28 us
    unnamed x2, local copies, waits for them, and re-layouts  1.26 us

profile of v6, /device:TPU:1, one launch (start us, length us, event | category | flops | bytes accessed | tf_op | source)
XLA Modules:
  0.0 31.1 jit_solution(16174048743103955167)
XLA Ops:
  1.9 28.0 %traction.1 = (f32[64,288]{1,0:T(8,128)S(1)}, f32[64,96]{1,0:T(8,128)S(1)}) custom-call(s32[1]{0:T(128)S(6)} %copy.14.near_count, s32[1]{0:T(128)S(6)} %copy.15.far_count, f32[64,288]{1,0:T(8,128)} %disp_hbm.1, f32[64,288]{1,0:T(8,128)} %pos_hbm.1, s32[2,256]{1,0:T(2,128)} %bitcast.7, s32[2,1024]{1,0:T(2,128)} %bitcast.6, s32[64,96]{1,0:T(8,128)} %intact_hbm.1, ...), custom_call_target="tpu_custom_call" | custom-call | tf_op jit(solution)/shard_map/traction/pallas_call | solution.py:450
  29.9 0.6 %copy.16 = f32[64,288]{1,0:T(8,128)} copy(f32[64,288]{1,0:T(8,128)S(1)} %get-tuple-element.4) | data formatting | bytes 147456
  30.5 0.6 %copy.17 = f32[64,96]{1,0:T(8,128)} copy(f32[64,96]{1,0:T(8,128)S(1)} %get-tuple-element.5) | data formatting | bytes 49152

commit v7 on v6

--- a/solution.py
+++ b/solution.py
@@ -18,6 +18,7 @@
 softening = 1.5
 
 PIECES = ((0, 0), (0, 1), (1, 0), (1, 1), (0, 2), (2, 0))
+PLAIN = (1,)
 SEEN = (range(0, 4), range(0, 5), range(1, 6), range(2, 6))
 
 
@@ -46,11 +47,14 @@
     centred,
     left,
     lefts,
+    held,
     sums,
     right_q,
     right_s,
     disp_rows,
     pos_rows,
+    disp_f,
+    pos_f,
     weights,
     near_rows,
     basis,
@@ -100,6 +104,9 @@
     for peer in peers:
         pl.semaphore_signal(barrier, inc=1, device_id=peer, device_id_type=LOGICAL)
 
+    for n in range(6):
+        wide[n, 0:8, :] = jnp.zeros((8, LANES), jnp.float32)
+        wide[n, OWN : OWN + 8, :] = jnp.zeros((8, LANES), jnp.float32)
     for copy in loads[:3]:
         copy.wait()
 
@@ -176,6 +183,8 @@
                     for n, (_, b) in enumerate(PIECES):
                         right_q[w, block_of(3 * n + c), :] = -2.0 * y_parts[c][b]
                         right_s[w, block_of(3 * n + c), :] = u_parts[c][b]
+                    disp_f[w, block_of(c), :] = u[c]
+                    pos_f[w, block_of(c), :] = 3.0 * y[c]
                     triple = thirds(3.0 * y[c])
                     for n in range(2):
                         disp_rows[w, block_of(4 * n + c), :] = u_parts[c][n]
@@ -189,7 +198,6 @@
                     disp_rows[w, block_of(n), :] = none
                     pos_rows[w, block_of(n), :] = 3.0 * one if n == 3 else none
 
-    wide[...] = jnp.zeros_like(wide)
     build(False)
 
     slots = near_pairs.shape[1]
@@ -223,50 +231,75 @@
             for c in range(3):
                 near_rows[c, row, 0:ELEMS] = total[c : c + 1] - centred[c, row, 0:ELEMS] * total[3:4]
 
-    turn(0)
-    turn(1)
+    def meet(g, w):
+        group = pl.ds(g, 24, stride=GROUPS)
+        right = jnp.concatenate([right_q[w, group, :], right_s[w, group, :]], axis=1).astype(bf16)
+        seen = [m for m in range(4) if w in SEEN[m]]
+        mine = jnp.concatenate([lefts[4 * g + m] for m in seen], axis=0)
+        both = jnp.dot(mine, right, preferred_element_type=f32)
+        for at, m in enumerate(seen):
+            held[6 * m + w] = both[at * ELEMS : (at + 1) * ELEMS]
 
     def near_groups(first, last):
-        def near_group(g, _):
-            group = pl.ds(g, 24, stride=GROUPS)
+        def near_group(t, _):
+            g = lax.rem(t + 1, GROUPS)
             eight = pl.ds(g, 8, stride=GROUPS)
-            rows, boths = [], []
+            rows = []
             for w in range(6):
-                right = jnp.concatenate([right_q[w, group, :], right_s[w, group, :]], axis=1).astype(bf16)
                 u_rows = disp_rows[w, eight, :].astype(bf16)
                 y_rows = pos_rows[w, eight, :].astype(bf16)
                 rows.append(jnp.concatenate([u_rows, u_rows, y_rows, y_rows], axis=1))
-                seen = [m for m in range(4) if w in SEEN[m]]
-                mine = jnp.concatenate([lefts[4 * g + m] for m in seen], axis=0)
-                both = jnp.dot(mine, right, preferred_element_type=f32)
-                boths.append({m: both[at * ELEMS : (at + 1) * ELEMS] for at, m in enumerate(seen)})
             totals = [None] * 4
+            plain = {m: [jnp.zeros((ELEMS, LANES), f32)] * 4 for m in PLAIN}
             for n in range(5):
                 for pair in range(2):
                     w = n + pair
                     seen = [m for m in (2 * pair, 2 * pair + 1) if w in SEEN[m]]
                     values = []
                     for m in seen:
-                        part = boths[w][m]
+                        part = held[6 * m + w]
                         inverse = lax.rsqrt(jnp.maximum(part[:, :LANES], core_square))
                         square = inverse * inverse
                         cube = square * (inverse * weights[w, pl.ds(4 * g + m, 1), :])
                         pull = (part[:, LANES:] * square) * cube
-                        values.append(jnp.concatenate(halves(cube) + halves(pull), axis=1))
+                        if m in PLAIN:
+                            u = [disp_f[w, pl.ds(GROUPS * c + g, 1), :] for c in range(3)]
+                            y = [pos_f[w, pl.ds(GROUPS * c + g, 1), :] for c in range(3)]
+                            plain[m] = [plain[m][c] + (cube * u[c] + pull * y[c]) for c in range(3)] + [plain[m][3] + pull]
+                        else:
+                            values.append(jnp.concatenate(halves(cube) + halves(pull), axis=1))
+                    seen = [m for m in seen if m not in PLAIN]
+                    if not seen:
+                        continue
                     added = lax.dot_general(
                         jnp.concatenate(values, axis=0), rows[w], (((1,), (1,)), ((), ())), preferred_element_type=f32
                     )
                     for at, m in enumerate(seen):
                         piece = added[at * ELEMS : (at + 1) * ELEMS]
                         totals[m] = piece if totals[m] is None else totals[m] + piece
-            settle(jnp.maximum(g - 1, 0))
+                meet(lax.rem(t + 2, GROUPS), n)
+            meet(lax.rem(t + 2, GROUPS), 5)
+            lane = lax.broadcasted_iota(jnp.int32, (ELEMS, 8), 1)
+            for m in PLAIN:
+                columns = [jnp.sum(x, axis=1, keepdims=True) for x in plain[m]]
+                columns[3] = 3.0 * columns[3]
+                total = jnp.zeros((ELEMS, 8), f32)
+                for c in range(4):
+                    total = jnp.where(lane == c, columns[c], total)
+                totals[m] = total
+            settle(t)
             for m in range(4):
                 sums[4 * g + m] = totals[m]
-            turn(jnp.minimum(g + 1, GROUPS - 1))
+            turn(lax.rem(t + 3, GROUPS))
             return 0
 
         lax.fori_loop(first, last, near_group, 0)
-        settle(last - 1)
+        settle(lax.rem(last, GROUPS))
+
+    turn(1)
+    turn(2)
+    for w in range(6):
+        meet(1, w)
 
     loads[3].wait()
 
@@ -292,9 +325,9 @@
     column[own_rows, :] = pack(coeff)
 
     z = lax.rem(j, 4) * 2 + i // (n_rows // 2)
-    sent = 8 - jnp.minimum(z, 4) * 3 // 2
-    gathered_at = sent + jnp.where(z == 0, 4, 5)
-    near_groups(1, sent)
+    sent = jnp.where(z == 0, 7, jnp.where(z == 1, 6, jnp.where(z == 2, 4, jnp.where(z == 3, 3, 0))))
+    gathered_at = sent + jnp.where(z < 2, 6, 5)
+    near_groups(0, sent)
     pl.semaphore_wait(barrier, len(peers))
 
     def remote(src, dst, send, recv, peer):
@@ -398,7 +431,6 @@
     ext_disp[120:128, :] = jnp.where(me == 0, 0.0, ext_disp[120:128, :])
     build(True)
     near_groups(gathered_at, GROUPS)
-    near_groups(0, 1)
 
     parts = [near_rows[c, :, 0:ELEMS] for c in range(3)]
     u = [ext_disp[0:OWN, lanes_of(c)] for c in range(3)]
@@ -466,11 +498,14 @@
             pltpu.VMEM((3, OWN, LANES), f32),
             pltpu.VMEM((4, 24 * GROUPS, LANES), f32),
             pltpu.VMEM((OWN, ELEMS, 24), bf16),
+            pltpu.VMEM((24, ELEMS, 2 * LANES), f32),
             pltpu.VMEM((OWN, ELEMS, 8), f32),
             pltpu.VMEM((6, 24 * GROUPS, LANES), f32),
             pltpu.VMEM((6, 24 * GROUPS, LANES), f32),
             pltpu.VMEM((6, 8 * GROUPS, LANES), f32),
             pltpu.VMEM((6, 8 * GROUPS, LANES), f32),
+            pltpu.VMEM((6, 3 * GROUPS, LANES), f32),
+            pltpu.VMEM((6, 3 * GROUPS, LANES), f32),
             pltpu.VMEM((6, OWN, LANES), f32),
             pltpu.VMEM((3, OWN, LANES), f32),
             pltpu.VMEM((OWN, RANK, WIDTH), bf16),
@@ -488,7 +523,7 @@
             pltpu.SemaphoreType.DMA((n_cols - 1,)),
         ],
         compiler_params=pltpu.CompilerParams(
-            collective_id=0, has_side_effects=True, vmem_limit_bytes=34 * 1024 * 1024
+            collective_id=0, has_side_effects=True, vmem_limit_bytes=40 * 1024 * 1024
         ),
         name="traction",
     )(

time: 31.2 us -> 30 us (0.962)
  Pallas kernels: 28 us -> 26.7 us
    pallas_call x1, Pallas kernels: 28 us -> 26.7 us  [local(): pl.pallas_call(functools.partial(mega, n_rows, n_cols), out_shape=(jax.Sh...]
where the time goes in v7:
time: 30 us; the launch traced here: 29.9 us
  Pallas kernels  26.7 us (89%)
  between operations  1.93 us (6%)
  local copies, waits for them, and re-layouts  1.26 us (4%)
    pallas_call x1, Pallas kernels, local(): pl.pallas_call(functools.partial(mega, n_rows, n_cols), out_shape=(jax.Sh...  26.7 us
    unnamed x2, local copies, waits for them, and re-layouts  1.26 us

profile of v7, /device:TPU:1, one launch (start us, length us, event | category | flops | bytes accessed | tf_op | source)
XLA Modules:
  0.0 29.9 jit_solution(8470709095197675635)
XLA Ops:
  1.9 26.7 %traction.1 = (f32[64,288]{1,0:T(8,128)S(1)}, f32[64,96]{1,0:T(8,128)S(1)}) custom-call(s32[1]{0:T(128)S(6)} %copy.14.near_count, s32[1]{0:T(128)S(6)} %copy.15.far_count, f32[64,288]{1,0:T(8,128)} %disp_hbm.1, f32[64,288]{1,0:T(8,128)} %pos_hbm.1, s32[2,256]{1,0:T(2,128)} %bitcast.7, s32[2,1024]{1,0:T(2,128)} %bitcast.6, s32[64,96]{1,0:T(8,128)} %intact_hbm.1, ...), custom_call_target="tpu_custom_call" | custom-call | tf_op jit(solution)/shard_map/traction/pallas_call | solution.py:482
  28.7 0.6 %copy.16 = f32[64,288]{1,0:T(8,128)} copy(f32[64,288]{1,0:T(8,128)S(1)} %get-tuple-element.4) | data formatting | bytes 147456
  29.3 0.6 %copy.17 = f32[64,96]{1,0:T(8,128)} copy(f32[64,96]{1,0:T(8,128)S(1)} %get-tuple-element.5) | data formatting | bytes 49152

commit v8 on v7

--- a/solution.py
+++ b/solution.py
@@ -325,8 +325,8 @@
     column[own_rows, :] = pack(coeff)
 
     z = lax.rem(j, 4) * 2 + i // (n_rows // 2)
-    sent = jnp.where(z == 0, 7, jnp.where(z == 1, 6, jnp.where(z == 2, 4, jnp.where(z == 3, 3, 0))))
-    gathered_at = sent + jnp.where(z < 2, 6, 5)
+    sent = jnp.where(z == 0, 8, jnp.where(z == 1, 6, jnp.where(z == 2, 4, jnp.where(z == 3, 3, 0))))
+    gathered_at = sent + jnp.where(z == 1, 6, 5)
     near_groups(0, sent)
     pl.semaphore_wait(barrier, len(peers))
 

time: 30 us -> 30.1 us (level)
  no operation moved by 1% of the time
where the time goes in v8:
time: 30.1 us; the launch traced here: 30 us
  Pallas kernels  26.8 us (89%)
  between operations  1.93 us (6%)
  local copies, waits for them, and re-layouts  1.26 us (4%)
    pallas_call x1, Pallas kernels, local(): pl.pallas_call(functools.partial(mega, n_rows, n_cols), out_shape=(jax.Sh...  26.8 us
    unnamed x2, local copies, waits for them, and re-layouts  1.26 us

profile of v8, /device:TPU:1, one launch (start us, length us, event | category | flops | bytes accessed | tf_op | source)
XLA Modules:
  0.0 30.0 jit_solution(13521688110410284505)
XLA Ops:
  1.9 26.8 %traction.1 = (f32[64,288]{1,0:T(8,128)S(1)}, f32[64,96]{1,0:T(8,128)S(1)}) custom-call(s32[1]{0:T(128)S(6)} %copy.14.near_count, s32[1]{0:T(128)S(6)} %copy.15.far_count, f32[64,288]{1,0:T(8,128)} %disp_hbm.1, f32[64,288]{1,0:T(8,128)} %pos_hbm.1, s32[2,256]{1,0:T(2,128)} %bitcast.7, s32[2,1024]{1,0:T(2,128)} %bitcast.6, s32[64,96]{1,0:T(8,128)} %intact_hbm.1, ...), custom_call_target="tpu_custom_call" | custom-call | tf_op jit(solution)/shard_map/traction/pallas_call | solution.py:482
  28.7 0.6 %copy.16 = f32[64,288]{1,0:T(8,128)} copy(f32[64,288]{1,0:T(8,128)S(1)} %get-tuple-element.4) | data formatting | bytes 147456
  29.4 0.6 %copy.17 = f32[64,96]{1,0:T(8,128)} copy(f32[64,96]{1,0:T(8,128)S(1)} %get-tuple-element.5) | data formatting | bytes 49152
